TPU v7x, 128 devices: a whole 4x4x4 slice. The times are simulated.
128 devices in a mesh: grp: 8 (over y_lo, z), tok: 16 (over y_hi, x, core).
Axes of the slice: x: 4, y: 4 (y_hi: 2, y_lo: 2; y = y_hi * 2 + y_lo), z: 4, core: 2. Of those that a mesh axis runs over, the one named last changes fastest.
Arguments:
- hidden: bfloat16 [8, 2048, 4608], P('grp', 'tok'), may hold values from -40 to 40
- input_gain: float32 [4608], replicated, may hold values from 0.25 to 1.75
- w_query: bfloat16 [4608, 4096], P(None, 'tok'), may hold values from -4 to 4
- w_key: bfloat16 [4608, 2048], P(None, 'tok'), may hold values from -4 to 4
- w_value: bfloat16 [4608, 2048], P(None, 'tok'), may hold values from -0.09375 to 0.09375
- w_out: bfloat16 [4096, 4608], P('tok'), may hold values from -0.09375 to 0.09375
- post_gain: float32 [4608], replicated, may hold values from 0.25 to 1.75
- cache_keys: bfloat16 [64, 256, 2048], P('grp', None, 'tok'), may hold values from -6 to 46
- cache_values: bfloat16 [64, 256, 2048], P('grp', None, 'tok'), may hold values from -6 to 6
- page_table: int32 [8, 8], replicated, may hold values from 0 to 63, as said below
- stretch_request: int32 [8, 8], P('grp'), may hold values from 0 to 2, never falling along the last dimension, each value on 1 to 4 neighbouring positions
- recompute_ids: int32 [8, 204], P('grp'), may hold values from 0 to 2047, as said below
- query_counts: int32 [8, 3], P('grp'), may hold values from 1 to 1024, 1844 in all within a row
Outputs:
- output: bfloat16 [8, 2048, 4608], P('grp', 'tok')
Inputs may be any that keep to these rules, and one draw needn't show every extreme that they name: `page_table`: row g lists the pages of group g's 8 stretch slots; page p is held by group p // 8; every page appears once, and the slots of a group take exactly one page from each group. `stretch_request`: each request of a group holds one or more consecutive slots, request numbers never fall along the slots, and one request holds (8 + 1) // 2 slots, none more. `recompute_ids`: each row holds 204 distinct cached tokens of the group (slot times 256 plus the token within the stretch) in rising order. `query_counts`: the counts of a group sum to 1844.
All inputs are finite; a program needn't handle non-finite values.
Results may differ from a plain program's by a relative error of at most 0.01.
Values may be sent and summed in bfloat16 or wider, within the bound.
A program may use at most 128 MiB of HBM per device.

v0:
```python
import math

import jax
import jax.numpy as jnp
from jax import lax
from jax.experimental import pallas as pl
from jax.experimental.pallas import tpu as pltpu
from jax.sharding import PartitionSpec as P

HEAD = 128
EPSILON = 1e-06
CAP_VALUE = 50.0
QUERY_SCALE = 1.0 / 12.0
ROPE_BASE = 10000.0
SPAN = 1 << 16
FAR = 1 << 30
BLOCK = 256


def angles_of(positions):
    halfway = HEAD // 2
    ladder = jnp.arange(halfway).astype(jnp.float32)
    frequency = jnp.exp(ladder * (-2.0 * math.log(ROPE_BASE) / HEAD))
    angles = positions.astype(jnp.float32)[:, None] * frequency[None, :]
    cosine = jnp.cos(angles)
    sine = jnp.sin(angles)
    return (
        jnp.concatenate([cosine, cosine], axis=1),
        jnp.concatenate([-sine, sine], axis=1),
    )


def request_layout(owners, counts_row, selected, table_row, groups, stretch_len, new_rows):
    slots = owners.shape[0]
    requests = counts_row.shape[0]
    request_ids = jnp.arange(requests, dtype=jnp.int32)
    slot_ids = jnp.arange(slots, dtype=jnp.int32)
    belongs = (owners[:, None] == request_ids[None, :]).astype(jnp.int32)
    first_slot = jnp.sum((owners[None, :] < request_ids[:, None]).astype(jnp.int32), axis=1)
    stretch_count = jnp.sum(belongs, axis=0)
    offsets = (slot_ids - jnp.sum(belongs * first_slot[None, :], axis=1)) * stretch_len
    home = ((selected // stretch_len)[:, None] == slot_ids[None, :]).astype(jnp.int32)
    select_req = jnp.sum(home * owners[None, :], axis=1)
    select_pos = jnp.sum(home * offsets[None, :], axis=1) + selected % stretch_len
    query_ids = jnp.arange(new_rows - selected.shape[0], dtype=jnp.int32)
    query_start = jnp.cumsum(counts_row) - counts_row
    query_req = jnp.sum((query_ids[:, None] >= query_start[None, 1:]).astype(jnp.int32), axis=1)
    mapping = (query_req[:, None] == request_ids[None, :]).astype(jnp.int32)
    query_pos = (
        jnp.sum(mapping * (stretch_count * stretch_len - query_start)[None, :], axis=1) + query_ids
    )
    row_req = jnp.concatenate([select_req, query_req])
    row_pos = jnp.concatenate([select_pos, query_pos])
    source = table_row // groups[1]
    place = (source[None, :] == jnp.arange(groups[0], dtype=jnp.int32)[:, None]).astype(jnp.int32)
    slot_of = jnp.sum(place * slot_ids[None, :], axis=1)
    shift_of = jnp.sum(place * offsets[None, :], axis=1)
    owner_of = jnp.sum(place * owners[None, :], axis=1)
    inner = jnp.arange(stretch_len, dtype=jnp.int32)
    cached_id = slot_of[:, None] * stretch_len + inner[None, :]
    cached_code = owner_of[:, None] * SPAN + shift_of[:, None] + inner[None, :]
    dead = jnp.any(cached_id.reshape(-1)[:, None] == selected[None, :], axis=1)
    row_code = row_req * SPAN + row_pos
    key_code = jnp.concatenate([cached_code.reshape(-1), row_code])
    live = jnp.concatenate([~dead, jnp.ones((new_rows,), bool)])
    return shift_of, row_req, row_pos, row_code, key_code, live


def attention_kernel(
    active, heads_ref, pk_ref, pv_ref, pcos_ref, psin_ref, rcode_ref, kcode_ref,
    live_ref, out_ref, keys, values, queries, total,
):
    rows = heads_ref.shape[1]
    cached = pk_ref.shape[0]
    blocks = rows // BLOCK
    for s in range(cached // BLOCK):
        part = pl.ds(s * BLOCK, BLOCK)
        page = pk_ref[part, :].astype(jnp.float32)
        turned = page * pcos_ref[s : s + 1, :] + pltpu.roll(page, HEAD // 2, 1) * psin_ref[s : s + 1, :]
        keys[part, :] = turned.astype(jnp.bfloat16)
        alive = live_ref[part, :].astype(jnp.bfloat16)
        values[part, :HEAD] = pv_ref[part, :] * alive
        values[part, HEAD:] = jnp.broadcast_to(alive, (BLOCK, HEAD))
    keys[pl.ds(cached, rows), :] = heads_ref[2]
    values[pl.ds(cached, rows), :HEAD] = heads_ref[3]
    values[pl.ds(cached, rows), HEAD:] = jnp.ones((rows, HEAD), jnp.bfloat16)

    def row_block(rb, carry):
        here = pl.ds(pl.multiple_of(rb * BLOCK, BLOCK), BLOCK)
        queries[:BLOCK, :] = heads_ref[0, here, :]
        queries[BLOCK:, :] = heads_ref[1, here, :]
        total[...] = jnp.zeros_like(total)
        code = rcode_ref[here, :]
        base = (code // SPAN) * SPAN

        def key_block(kb, inner_carry):
            @pl.when(active[rb, kb] > 0)
            def _():
                there = pl.ds(pl.multiple_of(kb * BLOCK, BLOCK), BLOCK)
                scores = lax.dot_general(
                    queries[...], keys[there, :], (((1,), (1,)), ((), ())),
                    preferred_element_type=jnp.float32,
                )
                capped = jnp.tanh(scores * (QUERY_SCALE / CAP_VALUE))
                weights = jnp.exp2(capped * (CAP_VALUE * math.log2(math.e)))
                kcode = kcode_ref[pl.ds(kb, 1), 0, :]
                seen = (kcode <= code) & (kcode >= base)
                both = jnp.concatenate([seen, seen], axis=0)
                rounded = jnp.where(both, weights, 0.0).astype(jnp.bfloat16)
                total[...] += jnp.dot(rounded, values[there, :], preferred_element_type=jnp.float32)

            return inner_carry

        lax.fori_loop(0, kcode_ref.shape[0], key_block, 0)
        result = total[:, :HEAD] / total[:, HEAD:]
        out_ref[here, :HEAD] = result[:BLOCK].astype(jnp.bfloat16)
        out_ref[here, HEAD:] = result[BLOCK:].astype(jnp.bfloat16)
        return carry

    lax.fori_loop(0, blocks, row_block, 0)


def attention(heads, page_k, page_v, pcos, psin, row_code, key_code, live):
    rows = heads.shape[1]
    total_keys = key_code.shape[0]
    key_blocks = key_code.reshape(-1, BLOCK)
    row_blocks = row_code.reshape(-1, BLOCK)
    low = jnp.min(key_blocks, axis=1)
    high = jnp.max(key_blocks, axis=1)
    row_high = jnp.max(row_blocks, axis=1)
    row_low = (jnp.min(row_blocks, axis=1) // SPAN) * SPAN
    active = ((low[None, :] <= row_high[:, None]) & (high[None, :] >= row_low[:, None])).astype(
        jnp.int32
    )
    vmem = pl.BlockSpec(memory_space=pltpu.VMEM)
    return pl.pallas_call(
        attention_kernel,
        out_shape=jax.ShapeDtypeStruct((rows, 2 * HEAD), jnp.bfloat16),
        in_specs=[pl.BlockSpec(memory_space=pltpu.SMEM)] + [vmem] * 8,
        out_specs=vmem,
        scratch_shapes=[
            pltpu.VMEM((total_keys, HEAD), jnp.bfloat16),
            pltpu.VMEM((total_keys, 2 * HEAD), jnp.bfloat16),
            pltpu.VMEM((2 * BLOCK, HEAD), jnp.bfloat16),
            pltpu.VMEM((2 * BLOCK, 2 * HEAD), jnp.float32),
        ],
        compiler_params=pltpu.CompilerParams(vmem_limit_bytes=40 << 20),
        name="attention",
    )(
        active, heads, page_k, page_v, pcos, psin, row_code[:, None],
        jnp.where(live, key_code, FAR).reshape(-1, 1, BLOCK), live.astype(jnp.float32)[: page_k.shape[0], None],
    )


MESH = pl.DeviceIdType.MESH
RINGS = 4
AROUND = 4


def place():
    tok = lax.axis_index("tok")
    return lax.axis_index("grp"), tok // 8, (tok // 2) % AROUND, tok % 2


def device(group, half, spot, core):
    return (group, half * 8 + lax.rem(spot + 2 * AROUND, AROUND) * 2 + core)


def greet(partners):
    barrier = pltpu.get_barrier_semaphore()
    for partner in partners:
        pl.semaphore_signal(barrier, inc=1, device_id=partner, device_id_type=MESH)
    pl.semaphore_wait(barrier, len(partners))


def project_kernel(
    attn_ref, w0_ref, w1_ref, hid_ref, gain_ref, out_ref,
    other, product, own, pair_out, pair_in, ring_out, ring_in, result,
    other_send, other_recv, pair_send, pair_recv, ring_send, ring_recv,
):
    group, half, spot, core = place()
    rows = hid_ref.shape[0]
    width = hid_ref.shape[1] // RINGS
    chunk = 2 * rows
    across = device(group, 1 - half, spot, core)
    sibling = device(group, half, spot, 1 - core)
    greet([across, sibling, device(group, half, spot + 1, core), device(group, half, spot - 1, core)])

    def other_copy(j):
        owner = lax.rem(spot + (3, 1, 2, 0)[j], AROUND)
        start = pl.multiple_of(((1 - half) * AROUND + owner) * chunk, chunk)
        return pltpu.make_async_remote_copy(
            src_ref=attn_ref.at[pl.ds(start, chunk)], dst_ref=other.at[j],
            send_sem=other_send.at[j], recv_sem=other_recv.at[j],
            device_id=across, device_id_type=MESH,
        )

    def pair_copy(s, r):
        return pltpu.make_async_remote_copy(
            src_ref=pair_out.at[s, r], dst_ref=pair_in.at[s, r],
            send_sem=pair_send.at[s, r], recv_sem=pair_recv.at[s, r],
            device_id=sibling, device_id_type=MESH,
        )

    def ring_copy(s, r):
        return pltpu.make_async_remote_copy(
            src_ref=ring_out.at[s, r], dst_ref=ring_in.at[s, r],
            send_sem=ring_send.at[s, r], recv_sem=ring_recv.at[s, r],
            device_id=device(group, half, spot + 1 - 2 * (r // 2), core), device_id_type=MESH,
        )

    for j in range(4):
        other_copy(j).start()

    def partial(s, r):
        owner = lax.rem(spot + (2 * (r // 2) - 1) * (1 + s) + 2 * AROUND, AROUND)
        slot = (r // 2, 2, 1 - r // 2, 3)[s]
        start = pl.multiple_of((half * AROUND + owner) * chunk, chunk)
        columns = pl.ds(pl.multiple_of(r * width, width), width)
        product[...] = jnp.dot(
            attn_ref[pl.ds(start, chunk), :], w0_ref[:, columns], preferred_element_type=jnp.float32
        ) + jnp.dot(other[slot], w1_ref[:, columns], preferred_element_type=jnp.float32)
        theirs = pl.ds(pl.multiple_of((1 - core) * rows, rows), rows)
        pair_out[s, r] = product[theirs, :].astype(jnp.bfloat16)
        pair_copy(s, r).start()
        own[s, r] = product[pl.ds(pl.multiple_of(core * rows, rows), rows), :]

    def partials(s, first, last):
        def step(r, carry):
            partial(s, r)
            return carry

        lax.fori_loop(first, last, step, 0)

    def forward(s):
        def step(r, carry):
            pair_copy(s, r).wait_recv()
            running = own[s, r] + pair_in[s, r].astype(jnp.float32)
            if s > 0:
                ring_copy(s - 1, r).wait_recv()
                running = running + ring_in[s - 1, r].astype(jnp.float32)
            if s < 3:
                ring_out[s, r] = running.astype(jnp.bfloat16)
                ring_copy(s, r).start()
            else:
                result[:, pl.ds(pl.multiple_of(r * width, width), width)] = running
            return carry

        for r in (0, 2, 1, 3):
            step(r, 0)

    other_copy(0).wait_recv()
    partials(0, 0, 2)
    other_copy(1).wait_recv()
    partials(0, 2, 4)
    forward(0)
    other_copy(2).wait_recv()
    partials(1, 0, 4)
    partials(2, 0, 4)
    other_copy(3).wait_recv()
    partials(3, 0, 4)
    forward(1)
    forward(2)
    forward(3)
    for j in range(4):
        other_copy(j).wait_send()

    def drain(r, carry):
        for s in range(4):
            pair_copy(s, r).wait_send()
        for s in range(3):
            ring_copy(s, r).wait_send()
        return carry

    lax.fori_loop(0, RINGS, drain, 0)
    projected = result[...]
    scale = lax.rsqrt(jnp.mean(projected * projected, axis=-1, keepdims=True) + EPSILON)
    out_ref[...] = (
        hid_ref[...].astype(jnp.float32) + projected * scale * gain_ref[...]
    ).astype(jnp.bfloat16)


def project(attended, w_own, w_across, own_rows, post_gain):
    rows, features = own_rows.shape
    width = features // RINGS
    vmem = pl.BlockSpec(memory_space=pltpu.VMEM)
    dma = pltpu.SemaphoreType.DMA
    return pl.pallas_call(
        project_kernel,
        out_shape=jax.ShapeDtypeStruct((rows, features), jnp.bfloat16),
        in_specs=[vmem] * 5,
        out_specs=vmem,
        scratch_shapes=[
            pltpu.VMEM((4, 2 * rows, attended.shape[1]), jnp.bfloat16),
            pltpu.VMEM((2 * rows, width), jnp.float32),
            pltpu.VMEM((4, RINGS, rows, width), jnp.float32),
            pltpu.VMEM((4, RINGS, rows, width), jnp.bfloat16),
            pltpu.VMEM((4, RINGS, rows, width), jnp.bfloat16),
            pltpu.VMEM((3, RINGS, rows, width), jnp.bfloat16),
            pltpu.VMEM((3, RINGS, rows, width), jnp.bfloat16),
            pltpu.VMEM((rows, features), jnp.float32),
            dma((4,)), dma((4,)), dma((4, RINGS)), dma((4, RINGS)), dma((3, RINGS)), dma((3, RINGS)),
        ],
        compiler_params=pltpu.CompilerParams(
            collective_id=1, has_side_effects=True, vmem_limit_bytes=56 << 20
        ),
        name="project",
    )(attended, w_own, w_across, own_rows, post_gain[None, :])


def project_in_kernel(
    hid_ref, gain_ref, wq_ref, wk_ref, wv_ref, cos_ref, sin_ref, wo_ref,
    heads_ref, wo_across_ref,
    normed, weights, ship,
    x_send, x_recv, f_send, f_recv, s_send, s_recv, y_send, y_recv, w_send, w_recv, z_send, z_recv,
    g_send, g_recv, o_send, o_recv, e_send, e_recv,
):
    group, half, spot, core = place()
    rows, features = hid_ref.shape
    depth = group % AROUND
    lows = group // AROUND
    quarter = features // 4
    out_quarter = wo_ref.shape[0] // 4

    def around(value):
        return lax.rem(value + 2 * AROUND, AROUND)

    xs = [device(group, half, spot + 1, core), device(group, half, spot - 1, core)]
    zs = [
        device(lows * AROUND + around(depth + 1), half, spot, core),
        device(lows * AROUND + around(depth - 1), half, spot, core),
    ]
    near = device((1 - lows) * AROUND + depth, 1 - half, spot, core)
    across = device(group, 1 - half, spot, core)
    beside = device((1 - lows) * AROUND + depth, half, spot, core)
    sibling = device(group, half, spot, 1 - core)
    greet(xs + zs + [near, across, beside, sibling])

    def copy(src, dst, send, recv, to):
        return pltpu.make_async_remote_copy(
            src_ref=src, dst_ref=dst, send_sem=send, recv_sem=recv, device_id=to, device_id_type=MESH
        )

    mine = pl.multiple_of(core * rows, rows)
    twin = pl.multiple_of((1 - core) * rows, rows)

    def block(owner, start=0, size=rows, base=mine):
        return normed.at[owner, pl.ds(pl.multiple_of(base + start, size), size)]

    def x_copy(d, owner=spot):
        return copy(block(owner), block(owner), x_send.at[d], x_recv.at[d], xs[d])

    def f_copy(d, owner):
        piece = block(owner, d * (rows // 2), rows // 2)
        return copy(piece, piece, f_send.at[d], f_recv.at[d], xs[d])

    def s_copy(i, owner, base=mine):
        piece = block(owner, base=base)
        return copy(piece, piece, s_send.at[i], s_recv.at[i], sibling)

    mine_first, theirs_first = 2 * lows, 2 * (1 - lows)

    def slab(q, p):
        return weights.at[q, pl.ds(pl.multiple_of(p * quarter, quarter), quarter)]

    def y_start(j):
        part = pl.ds(pl.multiple_of((theirs_first + j) * quarter, quarter), quarter)
        sources = [
            wq_ref.at[part, pl.ds(0, HEAD)], wq_ref.at[part, pl.ds(HEAD, HEAD)],
            wk_ref.at[part], wv_ref.at[part],
        ]
        for z, src in enumerate(sources):
            @pl.when(depth == z)
            def _(src=src):
                copy(src, slab(depth, theirs_first + j), y_send.at[j], y_recv.at[j], near).start()

    def y_done(j):
        piece = slab(depth, mine_first + j)
        return copy(piece, piece, y_send.at[j], y_recv.at[j], near)

    def w_copy(i, q, p):
        return copy(slab(q, p), slab(q, p), w_send.at[i], w_recv.at[i], beside)

    def nth_piece(n):
        return (mine_first if n < 2 else theirs_first) + n % 2

    def z_copy(d, n, q=depth):
        piece = slab(q, nth_piece(n))
        return copy(piece, piece, z_send.at[d, n], z_recv.at[d, n], zs[d])

    def g_copy(d, q):
        piece = slab(q, mine_first + d)
        return copy(piece, piece, g_send.at[d], g_recv.at[d], zs[d])

    def o_copy(i, src, q, n, to):
        size = out_quarter // 2
        part = pl.ds(pl.multiple_of(q * out_quarter + n * size, size), size)
        return copy(src.at[part], wo_across_ref.at[part], o_send.at[i], o_recv.at[i], to)

    def table(ref, owner):
        start = pl.multiple_of((half * AROUND + owner) * 2 * rows, 2 * rows)
        return ref[pl.ds(start, 2 * rows), :]

    def turned(u, cosine, sine):
        return u * cosine + pltpu.roll(u, HEAD // 2, 1) * sine

    def own_heads(owner):
        source = normed[owner]
        cosine, sine = table(cos_ref, owner), table(sin_ref, owner)
        to = pl.ds(pl.multiple_of((half * AROUND + owner) * 2 * rows, 2 * rows), 2 * rows)
        q = jnp.dot(source, wq_ref[...], preferred_element_type=jnp.float32)
        heads_ref[0, to] = turned(q[:, :HEAD], cosine, sine).astype(jnp.bfloat16)
        heads_ref[1, to] = turned(q[:, HEAD:], cosine, sine).astype(jnp.bfloat16)
        k = jnp.dot(source, wk_ref[...], preferred_element_type=jnp.float32)
        heads_ref[2, to] = turned(k, cosine, sine).astype(jnp.bfloat16)
        v = jnp.dot(source, wv_ref[...], preferred_element_type=jnp.float32)
        heads_ref[3, to] = v.astype(jnp.bfloat16)

    def e_copy(i, b, owner, q):
        to = pl.ds(pl.multiple_of((half * AROUND + owner) * 2 * rows, 2 * rows), 2 * rows)
        return copy(ship.at[i, b], heads_ref.at[q, to], e_send.at[i, b], e_recv.at[i, b], across)

    def nth(base, i):
        return around(base + (i * (7 - i)) // 2)

    owners = [nth(spot, b) for b in range(4)]
    quarters = [nth(depth, i) for i in range(4)]

    def their_heads(i, b):
        owner, q = nth(spot, b), nth(depth, i)
        u = jnp.dot(normed[owner], weights[q], preferred_element_type=jnp.float32)
        plain = (q == 3).astype(jnp.float32)
        cosine, sine = table(cos_ref, owner), table(sin_ref, owner)
        cosine = cosine + plain * (1.0 - cosine)
        sine = sine * (1.0 - plain)
        ship[i, b] = turned(u, cosine, sine).astype(jnp.bfloat16)
        e_copy(i, b, owner, q).start()

    def own_blocks(first, last):
        def step(b, carry):
            own_heads(nth(spot, b))
            return carry

        lax.fori_loop(first, last, step, 0)

    def their_blocks(i0, i1, b0, b1):
        def step(n, carry):
            their_heads(i0 + n // (b1 - b0), b0 + lax.rem(n, b1 - b0))
            return carry

        lax.fori_loop(0, (i1 - i0) * (b1 - b0), step, 0)

    left, right, far = owners[1], owners[2], owners[3]
    below, above, beyond = quarters[1], quarters[2], quarters[3]
    y_start(0)
    y_start(1)
    wide = hid_ref[...].astype(jnp.float32)
    scale = lax.rsqrt(jnp.mean(wide * wide, axis=-1, keepdims=True) + EPSILON)
    normed[spot, pl.ds(mine, rows)] = (wide * scale * gain_ref[...]).astype(jnp.bfloat16)
    x_copy(0).start()
    x_copy(1).start()
    s_copy(0, spot).start()
    for n in range(2):
        y_done(n).wait_recv()
        w_copy(n, depth, mine_first + n).start()
        z_copy(0, n).start()
        z_copy(1, n).start()
    o_copy(0, wo_ref, depth, 1 - lows, near).start()
    s_copy(0, spot, twin).wait_recv()
    own_blocks(0, 1)
    for n in range(2):
        w_copy(n, depth, theirs_first + n).wait_recv()
        z_copy(0, n + 2).start()
        z_copy(1, n + 2).start()
    their_blocks(0, 1, 0, 1)
    z_copy(0, 0, below).wait_recv()
    g_copy(0, below).start()
    z_copy(1, 1, above).wait_recv()
    g_copy(1, above).start()
    o_copy(0, wo_ref, depth, lows, near).wait_recv()
    o_copy(1, wo_across_ref, depth, lows, beside).start()
    x_copy(0, left).wait_recv()
    f_copy(0, left).start()
    s_copy(1, left).start()
    x_copy(1, right).wait_recv()
    f_copy(1, right).start()
    s_copy(2, right).start()
    s_copy(1, left, twin).wait_recv()
    s_copy(2, right, twin).wait_recv()
    their_blocks(0, 1, 1, 3)
    for n in range(1, 4):
        z_copy(0, n, below).wait_recv()
    for n in (0, 2, 3):
        z_copy(1, n, above).wait_recv()
    g_copy(0, beyond).wait_recv()
    w_copy(2, beyond, mine_first).start()
    g_copy(1, beyond).wait_recv()
    w_copy(3, beyond, mine_first + 1).start()
    o_copy(1, wo_across_ref, depth, 1 - lows, beside).wait_recv()
    for n in range(2):
        o_copy(2 + n, wo_across_ref, depth, n, zs[0]).start()
        o_copy(4 + n, wo_across_ref, depth, n, zs[1]).start()
    their_blocks(1, 3, 0, 3)
    own_blocks(1, 3)
    w_copy(2, beyond, theirs_first).wait_recv()
    w_copy(3, beyond, theirs_first + 1).wait_recv()
    their_blocks(3, 4, 0, 3)
    f_copy(0, far).wait_recv()
    f_copy(1, far).wait_recv()
    s_copy(3, far).start()
    s_copy(3, far, twin).wait_recv()
    their_blocks(0, 4, 3, 4)
    o_copy(2, wo_across_ref, below, 0, zs[0]).wait_recv()
    o_copy(6, wo_across_ref, below, 0, zs[0]).start()
    o_copy(5, wo_across_ref, above, 1, zs[1]).wait_recv()
    o_copy(7, wo_across_ref, above, 1, zs[1]).start()
    own_blocks(3, 4)
    o_copy(3, wo_across_ref, below, 1, zs[0]).wait_recv()
    o_copy(4, wo_across_ref, above, 0, zs[1]).wait_recv()
    o_copy(6, wo_across_ref, beyond, 0, zs[0]).wait_recv()
    o_copy(7, wo_across_ref, beyond, 1, zs[1]).wait_recv()
    for i in range(4):
        for b in range(4):
            to = pl.ds(
                pl.multiple_of(((1 - half) * AROUND + owners[b]) * 2 * rows, 2 * rows), 2 * rows
            )
            copy(
                ship.at[i, b], heads_ref.at[quarters[i], to], e_send.at[i, b], e_recv.at[i, b], across
            ).wait()
    for d in range(2):
        x_copy(d).wait_send()
        f_copy(d, owners[1 + d]).wait_send()
        for n in range(4):
            z_copy(d, n).wait_send()
        g_copy(d, quarters[1 + d]).wait_send()
    for i in range(4):
        s_copy(i, owners[i]).wait_send()
        w_copy(i, (depth, depth, beyond, beyond)[i], mine_first + i % 2).wait_send()
    for n in range(2):
        y_done(n).wait_send()
    for i in range(8):
        o_copy(i, wo_across_ref, depth, 0, near).wait_send()


def project_in(own_rows, gain, w_query, w_key, w_value, cosine, sine, w_out):
    rows, features = own_rows.shape
    vmem = pl.BlockSpec(memory_space=pltpu.VMEM)
    hbm = pl.BlockSpec(memory_space=pl.ANY)
    dma = pltpu.SemaphoreType.DMA
    pairs = [(2,), (2,), (4,), (2,), (4,), (2, 4), (2,), (8,), (4, 4)]
    return pl.pallas_call(
        project_in_kernel,
        out_shape=(
            jax.ShapeDtypeStruct((4, cosine.shape[0], HEAD), jnp.bfloat16),
            jax.ShapeDtypeStruct(w_out.shape, jnp.bfloat16),
        ),
        in_specs=[vmem] * 7 + [hbm],
        out_specs=(vmem, hbm),
        scratch_shapes=[
            pltpu.VMEM((AROUND, 2 * rows, features), jnp.bfloat16),
            pltpu.VMEM((4, features, HEAD), jnp.bfloat16),
            pltpu.VMEM((4, 4, 2 * rows, HEAD), jnp.bfloat16),
        ] + [dma(shape) for shape in pairs for _ in range(2)],
        compiler_params=pltpu.CompilerParams(
            collective_id=2, has_side_effects=True, vmem_limit_bytes=48 << 20
        ),
        name="project_in",
    )(own_rows, gain[None, :], w_query, w_key, w_value, cosine, sine, w_out)


def on_device(
    hidden, input_gain, w_query, w_key, w_value, w_out, post_gain, cache_keys, cache_values,
    page_table, stretch_request, recompute_ids, query_counts,
):
    own_rows = hidden[0]
    tok_total = lax.axis_size("tok")
    groups = lax.axis_size("grp")
    new_rows = own_rows.shape[0] * tok_total
    pages, stretch_len = cache_keys.shape[:2]
    group = lax.axis_index("grp")
    mine = page_table // pages == group
    local = jnp.sum(jnp.where(mine, page_table % pages, 0), axis=1)
    picks = (local[:, None] == jnp.arange(pages, dtype=jnp.int32)[None, :]).astype(jnp.bfloat16)
    both = jnp.concatenate([cache_keys, cache_values], axis=-1)
    send = jnp.einsum("gp,pkh->gkh", picks, both, preferred_element_type=jnp.float32).astype(
        jnp.bfloat16
    )
    got = lax.all_to_all(send, "grp", 0, 0, tiled=True)
    got = got.reshape(groups * stretch_len, 2 * HEAD)
    table_row = lax.dynamic_index_in_dim(page_table, group, 0, keepdims=False)
    shift_of, row_req, row_pos, row_code, key_code, live = request_layout(
        stretch_request[0], query_counts[0], recompute_ids[0], table_row, (groups, pages),
        stretch_len, new_rows,
    )
    pcos, psin = angles_of(shift_of)
    cosine, sine = angles_of(row_pos)
    heads, w_across = project_in(own_rows, input_gain, w_query, w_key, w_value, cosine, sine, w_out)
    attended = attention(
        heads, got[:, :HEAD], got[:, HEAD:], pcos, psin, row_code, key_code, live
    )
    output = project(attended, w_out, w_across, own_rows, post_gain)
    return output[None]


def solution(mesh):
    return jax.shard_map(
        on_device,
        mesh=mesh,
        in_specs=(
            P("grp", "tok", None), P(), P(None, "tok"), P(None, "tok"), P(None, "tok"),
            P("tok", None), P(), P("grp", None, "tok"), P("grp", None, "tok"), P(),
            P("grp", None), P("grp", None), P("grp", None),
        ),
        out_specs=P("grp", "tok", None),
        check_vma=False,
    )
```

profile of v0, /device:TPU:1, one launch (start us, length us, event | category | flops | bytes accessed | tf_op | source)
XLA Modules:
  0.0 203.1 jit_solution(2294076735655330201)
XLA Ops:
  0.0 0.0 copy-start.11
  0.0 1.4 copy.40
  1.4 1.4 copy.39
  2.8 0.0 copy-done.11
  2.8 0.1 fusion.12
  2.9 0.5 convolution_convert_fusion
  3.4 0.0 copy-start.12
  3.4 0.0 copy-start.10
  3.4 0.0 copy-start.9
  3.5 1.2 copy.41
  4.7 6.9 %all-to-all-start = ((bf16[8,256,256]{2,1,0:T(8,128)(2,1)}), bf16[8,256,256]{2,1,0:T(8,128)(2,1)}, u32[]{:S(2)}, u32[]{:S(2)}) async-start(bf16[8,256,256]{2,1,0:T(8,128)(2,1)} %copy.41), calls=%async_computation | async-start | bytes 2097152 | tf_op jit(solution)/shard_map/all_to_all | solution.py:588
  11.6 0.0 copy-done.12
  11.6 0.2 reduce-window.4
  11.7 0.0 copy-done.10
  11.7 0.1 convert_reduce_fusion.1
  11.9 0.1 select_reduce_fusion.6
  12.0 0.1 slice.11
  12.1 0.1 fusion.4
  12.2 0.1 select_reduce_fusion
  12.3 0.0 copy-done.9
  12.3 0.1 select_reduce_fusion.1
  12.5 0.1 select_reduce_fusion.3
  12.6 0.1 fusion.17
  12.7 0.1 fusion.9
  12.8 3.7 %fusion.3 = (f32[2048,64]{1,0:T(8,128)S(1)}, f32[2048,64]{1,0:T(8,128)S(1)}, f32[2048,64]{1,0:T(8,128)S(1)}) fusion(f32[64]{0:T(128)S(1)} %multiply_exponential_fusion, f32[2048]{0:T(1024)S(1)} %get-tuple-element.22), kind=kLoop, calls=%fused_computation.9 | loop fusion | flops 262144 | bytes 1581312 | tf_op jit(solution)/shard_map/neg | solution.py:29
  16.5 0.1 fusion.20
  16.6 0.1 add_bitcast_fusion
  16.7 0.3 compare_reduce_fusion
  17.0 0.0 copy-start.7
  17.0 1.9 pad_maximum_fusion
  19.0 0.0 copy-start.8
  19.0 0.0 copy-start
  19.0 0.1 fusion.8
  19.1 0.0 copy-done.7
  19.1 0.4 copy.42.rcode_ref
  19.5 0.4 copy.43.live_ref
  19.9 0.0 copy-done.8
  19.9 0.6 broadcast_in_dim.19.gain_ref
  20.5 0.0 copy-done
  20.5 0.0 copy-start.2
  20.5 1.2 copy-done.2
  21.7 0.0 copy-start.3
  21.7 1.2 copy-done.3
  23.0 0.0 copy-start.5
  23.0 1.3 copy-done.5
  24.2 0.0 copy-start.6
  24.2 1.3 copy-done.6
  25.5 80.3 %project_in.1 = (bf16[4,2048,128]{2,1,0:T(8,128)(2,1)}, bf16[256,4608]{1,0:T(8,128)(2,1)}) custom-call(bf16[128,4608]{1,0:T(8,128)(2,1)S(1)} %bitcast.36, f32[1,4608]{1,0:T(1,128)S(1)} %broadcast_in_dim.15.gain_ref, bf16[4608,256]{1,0:T(8,128)(2,1)} %wq_ref.1, bf16[4608,128]{1,0:T(8,128)(2,1)S(1)} %copy-done.5, bf16[4608,128]{1,0:T(8,128)(2,1)S(1)} %copy-done.6, ...), custom_call_target="tpu_custom_call" | custom-call | tf_op jit(solution)/shard_map/project_in/pallas_call | solution.py:551
  105.9 0.1 fusion.6
  106.0 0.1 pad_maximum_fusion.2.pcos_ref
  106.1 0.1 pad_maximum_fusion.3.psin_ref
  106.1 0.1 fusion.26
  106.3 0.1 and_convert_fusion.active
  106.4 0.0 all-to-all-done
  106.4 0.0 copy-start.4
  106.4 1.4 fusion.27
  107.8 0.5 copy-done.4
  108.3 31.1 %attention.1.attn_ref = bf16[2048,256]{1,0:T(8,128)(2,1)S(1)} custom-call(s32[8,16]{1,0:T(8,128)S(1)} %and_convert_fusion.active, bf16[4,2048,128]{2,1,0:T(8,128)(2,1)S(1)} %copy-done.4, bf16[2048,128]{1,0:T(8,128)(2,1)S(1)} %get-tuple-element.21.pk_ref, bf16[2048,128]{1,0:T(8,128)(2,1)S(1)} %get-tuple-element.20.pv_ref, ...), custom_call_target="tpu_custom_call" | custom-call | tf_op jit(solution)/shard_map/attention/pallas_call | solution.py:136
  139.4 0.0 copy-start.1
  139.4 1.0 copy-done.1
  140.4 60.3 %project.1 = bf16[128,4608]{1,0:T(8,128)(2,1)} custom-call(bf16[2048,256]{1,0:T(8,128)(2,1)} %copy-done.1, bf16[256,4608]{1,0:T(8,128)(2,1)} %w0_ref.1, bf16[256,4608]{1,0:T(8,128)(2,1)} %get-tuple-element.8.w1_ref, bf16[128,4608]{1,0:T(8,128)(2,1)} %bitcast.35, f32[1,4608]{1,0:T(1,128)} %broadcast_in_dim.19.gain_ref), custom_call_target="tpu_custom_call" | custom-call | tf_op jit(solution)/shard_map/project/pallas_call | solution.py:288
  200.7 2.4 %copy.47 = bf16[1,128,4608]{2,1,0:T(8,128)(2,1)} copy(bf16[1,128,4608]{2,1,0:T(8,128)(2,1)} %bitcast.38) | data formatting | bytes 2359296
  (18 shorter events, 0.1 us)
Async XLA Ops:
  0.0 2.8 %copy-start.11 = (s32[8,8]{1,0:T(8,128)S(1)}, s32[8,8]{1,0:T(8,128)}, u32[]{:S(2)}) copy-start(s32[8,8]{1,0:T(8,128)} %param.22) | copy-start | bytes 772
  3.4 8.1 %copy-start.12 = (s32[1,3]{1,0:T(1,128)S(1)}, s32[1,3]{1,0:T(1,128)}, u32[]{:S(2)}) copy-start(s32[1,3]{1,0:T(1,128)} %param.25) | copy-start | bytes 40
  3.4 8.3 %copy-start.10 = (s32[1,8]{1,0:T(1,128)S(1)}, s32[1,8]{1,0:T(1,128)}, u32[]{:S(2)}) copy-start(s32[1,8]{1,0:T(1,128)} %param.23) | copy-start | bytes 100
  3.4 8.9 %copy-start.9 = (s32[1,204]{1,0:T(1,128)S(1)}, s32[1,204]{1,0:T(1,128)}, u32[]{:S(2)}) copy-start(s32[1,204]{1,0:T(1,128)} %param.24) | copy-start | bytes 2452
  4.7 101.7 %all-to-all-start = ((bf16[8,256,256]{2,1,0:T(8,128)(2,1)}), bf16[8,256,256]{2,1,0:T(8,128)(2,1)}, u32[]{:S(2)}, u32[]{:S(2)}) async-start(bf16[8,256,256]{2,1,0:T(8,128)(2,1)} %copy.41), calls=%async_computation | async-start | bytes 2097152 | tf_op jit(solution)/shard_map/all_to_all | solution.py:588
  17.0 2.1 %copy-start.7 = (f32[4608]{0:T(1024)S(1)}, f32[4608]{0:T(1024)}, u32[]{:S(2)}) copy-start(f32[4608]{0:T(1024)} %param.14) | copy-start | bytes 55300
  19.0 0.9 copy-start.8
  19.0 1.5 copy-start
  20.5 1.2 copy-start.2
  21.7 1.2 copy-start.3
  23.0 1.3 copy-start.5
  24.2 1.3 copy-start.6
  106.4 1.9 copy-start.4
  139.4 1.0 copy-start.1
where the time goes:
time: 204 us; the launch traced here: 203 us
  Pallas kernels  172 us (84%)
  local copies, waits for them, and re-layouts  15.7 us (8%)
  other arithmetic  7.95 us (4%)
  starting transfers between devices  6.87 us (3%)
    pallas_call x1, Pallas kernels, project_in(): pl.pallas_call(project_in_kernel, out_shape=(jax.ShapeDtypeStruct((4, cos...  80.3 us
    pallas_call x1, Pallas kernels, project(): pl.pallas_call(project_kernel, out_shape=jax.ShapeDtypeStruct((rows, feat...  60.3 us
    pallas_call x1, Pallas kernels, attention(): pl.pallas_call(attention_kernel, out_shape=jax.ShapeDtypeStruct((rows, 2...  31.1 us
    unnamed x31, local copies, waits for them, and re-layouts  11.6 us
    all_to_all x1, starting transfers between devices, on_device(): got = lax.all_to_all(send, 'grp', 0, 0, tiled=True)  6.87 us
  transfers between devices with their start and end apart: 1, of which 0 were waited for; matrix products, arithmetic and copies ran while one was open for 5% of the time, Pallas kernels for 40%

commit v1 on v0

--- a/solution.py
+++ b/solution.py
@@ -1,7 +1,9 @@
+import functools
 import math
 
 import jax
 import jax.numpy as jnp
+import numpy as np
 from jax import lax
 from jax.experimental import pallas as pl
 from jax.experimental.pallas import tpu as pltpu
@@ -14,141 +16,172 @@
 ROPE_BASE = 10000.0
 SPAN = 1 << 16
 FAR = 1 << 30
-BLOCK = 256
-
-
-def angles_of(positions):
-    halfway = HEAD // 2
-    ladder = jnp.arange(halfway).astype(jnp.float32)
-    frequency = jnp.exp(ladder * (-2.0 * math.log(ROPE_BASE) / HEAD))
-    angles = positions.astype(jnp.float32)[:, None] * frequency[None, :]
-    cosine = jnp.cos(angles)
-    sine = jnp.sin(angles)
-    return (
-        jnp.concatenate([cosine, cosine], axis=1),
-        jnp.concatenate([-sine, sine], axis=1),
-    )
-
-
-def request_layout(owners, counts_row, selected, table_row, groups, stretch_len, new_rows):
-    slots = owners.shape[0]
-    requests = counts_row.shape[0]
-    request_ids = jnp.arange(requests, dtype=jnp.int32)
-    slot_ids = jnp.arange(slots, dtype=jnp.int32)
-    belongs = (owners[:, None] == request_ids[None, :]).astype(jnp.int32)
-    first_slot = jnp.sum((owners[None, :] < request_ids[:, None]).astype(jnp.int32), axis=1)
-    stretch_count = jnp.sum(belongs, axis=0)
-    offsets = (slot_ids - jnp.sum(belongs * first_slot[None, :], axis=1)) * stretch_len
-    home = ((selected // stretch_len)[:, None] == slot_ids[None, :]).astype(jnp.int32)
-    select_req = jnp.sum(home * owners[None, :], axis=1)
-    select_pos = jnp.sum(home * offsets[None, :], axis=1) + selected % stretch_len
-    query_ids = jnp.arange(new_rows - selected.shape[0], dtype=jnp.int32)
-    query_start = jnp.cumsum(counts_row) - counts_row
-    query_req = jnp.sum((query_ids[:, None] >= query_start[None, 1:]).astype(jnp.int32), axis=1)
-    mapping = (query_req[:, None] == request_ids[None, :]).astype(jnp.int32)
-    query_pos = (
-        jnp.sum(mapping * (stretch_count * stretch_len - query_start)[None, :], axis=1) + query_ids
-    )
-    row_req = jnp.concatenate([select_req, query_req])
-    row_pos = jnp.concatenate([select_pos, query_pos])
-    source = table_row // groups[1]
-    place = (source[None, :] == jnp.arange(groups[0], dtype=jnp.int32)[:, None]).astype(jnp.int32)
-    slot_of = jnp.sum(place * slot_ids[None, :], axis=1)
-    shift_of = jnp.sum(place * offsets[None, :], axis=1)
-    owner_of = jnp.sum(place * owners[None, :], axis=1)
-    inner = jnp.arange(stretch_len, dtype=jnp.int32)
-    cached_id = slot_of[:, None] * stretch_len + inner[None, :]
-    cached_code = owner_of[:, None] * SPAN + shift_of[:, None] + inner[None, :]
-    dead = jnp.any(cached_id.reshape(-1)[:, None] == selected[None, :], axis=1)
-    row_code = row_req * SPAN + row_pos
-    key_code = jnp.concatenate([cached_code.reshape(-1), row_code])
-    live = jnp.concatenate([~dead, jnp.ones((new_rows,), bool)])
-    return shift_of, row_req, row_pos, row_code, key_code, live
+BLOCK = 512
+
+
+def frequencies():
+    ladder = np.arange(HEAD // 2, dtype=np.float32)
+    return np.exp(ladder * np.float32(-2.0 * math.log(ROPE_BASE) / HEAD)).astype(np.float32)
+
+
+def turned(u, cosine, sine):
+    return u * cosine + pltpu.roll(u, HEAD // 2, 1) * sine
+
+
+def request_base(code):
+    return jnp.where(code >= 2 * SPAN, 2 * SPAN, jnp.where(code >= SPAN, SPAN, 0))
+
+
+class Layout:
+    def __init__(self, owners, counts, stretch):
+        slots = owners.shape[0]
+        self.stretch = stretch
+        self.owners = [owners[c] for c in range(slots)]
+        held = [sum((o == r).astype(jnp.int32) for o in self.owners) for r in range(3)]
+        first = [0, held[0], held[0] + held[1]]
+        self.offsets = []
+        self.slot_bases = []
+        for c, o in enumerate(self.owners):
+            start = jnp.where(o == 0, first[0], jnp.where(o == 1, first[1], first[2]))
+            self.offsets.append(c - start)
+            self.slot_bases.append(o * SPAN - start * stretch)
+        self.starts = [0, counts[0], counts[0] + counts[1]]
+        self.query_bases = [r * SPAN + held[r] * stretch - self.starts[r] for r in range(3)]
+
+    def of_queries(self, m):
+        base = jnp.where(
+            m >= self.starts[2], self.query_bases[2],
+            jnp.where(m >= self.starts[1], self.query_bases[1], self.query_bases[0]),
+        )
+        return m + base
+
+    def of_cached(self, ids):
+        base = self.slot_bases[0]
+        for c in range(1, len(self.slot_bases)):
+            base = jnp.where(ids >= c * self.stretch, self.slot_bases[c], base)
+        return ids + base
+
+    def request_of(self, m):
+        return (m >= self.starts[1]).astype(jnp.int32) + (m >= self.starts[2]).astype(jnp.int32)
 
 
 def attention_kernel(
-    active, heads_ref, pk_ref, pv_ref, pcos_ref, psin_ref, rcode_ref, kcode_ref,
-    live_ref, out_ref, keys, values, queries, total,
+    selected, owners_ref, counts_ref, table_ref, heads_ref, pages_ref, pcos_ref, psin_ref,
+    ids_col_ref, ids_row_ref, out_ref, keys, values, key_codes, row_codes, row_bases, queries, total,
 ):
     rows = heads_ref.shape[1]
-    cached = pk_ref.shape[0]
-    blocks = rows // BLOCK
-    for s in range(cached // BLOCK):
-        part = pl.ds(s * BLOCK, BLOCK)
-        page = pk_ref[part, :].astype(jnp.float32)
-        turned = page * pcos_ref[s : s + 1, :] + pltpu.roll(page, HEAD // 2, 1) * psin_ref[s : s + 1, :]
-        keys[part, :] = turned.astype(jnp.bfloat16)
-        alive = live_ref[part, :].astype(jnp.bfloat16)
-        values[part, :HEAD] = pv_ref[part, :] * alive
-        values[part, HEAD:] = jnp.broadcast_to(alive, (BLOCK, HEAD))
+    groups, stretch = pages_ref.shape[:2]
+    cached = groups * stretch
+    group = lax.axis_index("grp")
+    layout = Layout(owners_ref, counts_ref, stretch)
+    lane = lax.broadcasted_iota(jnp.int32, (1, stretch), 1)
+    below = lax.broadcasted_iota(jnp.int32, (stretch, 1), 0)
+    ids_col = ids_col_ref[...]
+    per = BLOCK // stretch
+
+    def put_codes(i, codes):
+        key_codes[i // per, :, pl.ds((i % per) * stretch, stretch)] = codes
+
+    for c in range(groups):
+        page = table_ref[group, c]
+        source = page // (table_ref.shape[1])
+        part = pl.ds(c * stretch, stretch)
+        turn = layout.offsets[c]
+        k = pages_ref[source, :, :HEAD].astype(jnp.float32)
+        k = turned(k, pcos_ref[pl.ds(turn, 1), :], psin_ref[pl.ds(turn, 1), :])
+        keys[part, :] = k.astype(jnp.bfloat16)
+        values[part, :HEAD] = pages_ref[source, :, HEAD:]
+        ids = lane + c * stretch
+        dead = jnp.max((ids_col == ids).astype(jnp.int32), axis=0, keepdims=True)
+        put_codes(c, jnp.where(dead > 0, FAR, ids + layout.slot_bases[c]))
     keys[pl.ds(cached, rows), :] = heads_ref[2]
     values[pl.ds(cached, rows), :HEAD] = heads_ref[3]
-    values[pl.ds(cached, rows), HEAD:] = jnp.ones((rows, HEAD), jnp.bfloat16)
+    values[:, HEAD:] = jnp.ones((cached + rows, HEAD), jnp.bfloat16)
+    for i in range(rows // stretch):
+        by_lane = layout.of_queries(lane + (i * stretch - selected))
+        by_row = layout.of_queries(below + (i * stretch - selected))
+        if i == 0:
+            by_lane = jnp.where(lane < selected, layout.of_cached(ids_row_ref[...]), by_lane)
+            by_row = jnp.where(below < selected, layout.of_cached(ids_col), by_row)
+        put_codes(groups + i, by_lane)
+        row_codes[pl.ds(i * stretch, stretch), :] = by_row
+        row_bases[pl.ds(i * stretch, stretch), :] = request_base(by_row)
+
+    ahead = cached // BLOCK
 
     def row_block(rb, carry):
         here = pl.ds(pl.multiple_of(rb * BLOCK, BLOCK), BLOCK)
         queries[:BLOCK, :] = heads_ref[0, here, :]
         queries[BLOCK:, :] = heads_ref[1, here, :]
         total[...] = jnp.zeros_like(total)
-        code = rcode_ref[here, :]
-        base = (code // SPAN) * SPAN
+        code = row_codes[here, :]
+        base = row_bases[here, :]
+        low = jnp.where(rb == 0, 0, layout.request_of(rb * BLOCK - selected))
+        high = jnp.where(rb == 0, 2, layout.request_of(rb * BLOCK - selected + BLOCK - 1))
+
+        def attend(kb):
+            there = pl.ds(pl.multiple_of(kb * BLOCK, BLOCK), BLOCK)
+            scores = lax.dot_general(
+                queries[...], keys[there, :], (((1,), (1,)), ((), ())),
+                preferred_element_type=jnp.float32,
+            )
+            capped = jnp.tanh(scores * (QUERY_SCALE / CAP_VALUE))
+            weights = jnp.exp2(capped * (CAP_VALUE * math.log2(math.e)))
+            key_code = key_codes[kb]
+            seen = (key_code <= code) & (key_code >= base)
+            both = jnp.concatenate([seen, seen], axis=0)
+            rounded = jnp.where(both, weights, 0.0).astype(jnp.bfloat16)
+            total[...] += jnp.dot(rounded, values[there, :], preferred_element_type=jnp.float32)
 
         def key_block(kb, inner_carry):
-            @pl.when(active[rb, kb] > 0)
+            slot = jnp.minimum(kb * per, groups - per)
+            from_cache = (owners_ref[slot] <= high) & (owners_ref[slot + per - 1] >= low)
+            last = (kb - ahead + 1) * BLOCK - 1 - selected
+            from_new = (kb == ahead) | (layout.request_of(last) >= low)
+
+            @pl.when(((kb < ahead) & from_cache) | ((kb >= ahead) & from_new))
             def _():
-                there = pl.ds(pl.multiple_of(kb * BLOCK, BLOCK), BLOCK)
-                scores = lax.dot_general(
-                    queries[...], keys[there, :], (((1,), (1,)), ((), ())),
-                    preferred_element_type=jnp.float32,
-                )
-                capped = jnp.tanh(scores * (QUERY_SCALE / CAP_VALUE))
-                weights = jnp.exp2(capped * (CAP_VALUE * math.log2(math.e)))
-                kcode = kcode_ref[pl.ds(kb, 1), 0, :]
-                seen = (kcode <= code) & (kcode >= base)
-                both = jnp.concatenate([seen, seen], axis=0)
-                rounded = jnp.where(both, weights, 0.0).astype(jnp.bfloat16)
-                total[...] += jnp.dot(rounded, values[there, :], preferred_element_type=jnp.float32)
+                attend(kb)
 
             return inner_carry
 
-        lax.fori_loop(0, kcode_ref.shape[0], key_block, 0)
+        lax.fori_loop(0, ahead + rb + 1, key_block, 0)
         result = total[:, :HEAD] / total[:, HEAD:]
         out_ref[here, :HEAD] = result[:BLOCK].astype(jnp.bfloat16)
         out_ref[here, HEAD:] = result[BLOCK:].astype(jnp.bfloat16)
         return carry
 
-    lax.fori_loop(0, blocks, row_block, 0)
-
-
-def attention(heads, page_k, page_v, pcos, psin, row_code, key_code, live):
+    lax.fori_loop(0, rows // BLOCK, row_block, 0)
+
+
+def attention(heads, pages, owners, counts, table, selected, ids_col, ids_row):
     rows = heads.shape[1]
-    total_keys = key_code.shape[0]
-    key_blocks = key_code.reshape(-1, BLOCK)
-    row_blocks = row_code.reshape(-1, BLOCK)
-    low = jnp.min(key_blocks, axis=1)
-    high = jnp.max(key_blocks, axis=1)
-    row_high = jnp.max(row_blocks, axis=1)
-    row_low = (jnp.min(row_blocks, axis=1) // SPAN) * SPAN
-    active = ((low[None, :] <= row_high[:, None]) & (high[None, :] >= row_low[:, None])).astype(
-        jnp.int32
-    )
+    groups, stretch = pages.shape[:2]
+    total_keys = groups * stretch + rows
+    angles = (np.arange(groups, dtype=np.float32) * stretch)[:, None] * frequencies()[None, :]
+    cosine, sine = np.cos(angles), np.sin(angles)
     vmem = pl.BlockSpec(memory_space=pltpu.VMEM)
+    smem = pl.BlockSpec(memory_space=pltpu.SMEM)
     return pl.pallas_call(
-        attention_kernel,
+        functools.partial(attention_kernel, selected),
         out_shape=jax.ShapeDtypeStruct((rows, 2 * HEAD), jnp.bfloat16),
-        in_specs=[pl.BlockSpec(memory_space=pltpu.SMEM)] + [vmem] * 8,
+        in_specs=[smem] * 3 + [vmem] * 6,
         out_specs=vmem,
         scratch_shapes=[
             pltpu.VMEM((total_keys, HEAD), jnp.bfloat16),
             pltpu.VMEM((total_keys, 2 * HEAD), jnp.bfloat16),
+            pltpu.VMEM((total_keys // BLOCK, 1, BLOCK), jnp.int32),
+            pltpu.VMEM((rows, 1), jnp.int32),
+            pltpu.VMEM((rows, 1), jnp.int32),
             pltpu.VMEM((2 * BLOCK, HEAD), jnp.bfloat16),
             pltpu.VMEM((2 * BLOCK, 2 * HEAD), jnp.float32),
         ],
         compiler_params=pltpu.CompilerParams(vmem_limit_bytes=40 << 20),
         name="attention",
     )(
-        active, heads, page_k, page_v, pcos, psin, row_code[:, None],
-        jnp.where(live, key_code, FAR).reshape(-1, 1, BLOCK), live.astype(jnp.float32)[: page_k.shape[0], None],
+        owners, counts, table, heads, pages,
+        np.concatenate([cosine, cosine], axis=1), np.concatenate([-sine, sine], axis=1),
+        ids_col, ids_row,
     )
 
 
@@ -309,10 +342,11 @@
 
 
 def project_in_kernel(
-    hid_ref, gain_ref, wq_ref, wk_ref, wv_ref, cos_ref, sin_ref, wo_ref,
-    heads_ref, wo_across_ref,
-    normed, weights, ship,
-    x_send, x_recv, f_send, f_recv, s_send, s_recv, y_send, y_recv, w_send, w_recv, z_send, z_recv,
+    selected, owners_ref, counts_ref, table_ref, hid_ref, gain_ref, freq_ref, ids_ref,
+    wq_hbm, wk_hbm, wv_hbm, ck_hbm, cv_hbm, wo_ref,
+    heads_ref, wo_across_ref, pages_ref,
+    normed, weights, ship, wq_ref, wk_ref, wv_ref, ck_ref, cv_ref, outgoing, cos_ref, sin_ref,
+    l_sem, p_send, p_recv, x_send, x_recv, f_send, f_recv, s_send, s_recv, y_send, y_recv, w_send, w_recv, z_send, z_recv,
     g_send, g_recv, o_send, o_recv, e_send, e_recv,
 ):
     group, half, spot, core = place()
@@ -334,7 +368,23 @@
     across = device(group, 1 - half, spot, core)
     beside = device((1 - lows) * AROUND + depth, half, spot, core)
     sibling = device(group, half, spot, 1 - core)
-    greet(xs + zs + [near, across, beside, sibling])
+    offsets = [(0, 1), (0, -1), (1, 0), (0, 2), (1, 1), (1, -1), (1, 2)]
+
+    def group_at(low, deep):
+        return lax.rem(lows + low, 2) * AROUND + around(depth + deep)
+
+    local = [
+        pltpu.make_async_copy(src, dst, l_sem.at[i])
+        for i, (src, dst) in enumerate(
+            [(ck_hbm, ck_ref), (cv_hbm, cv_ref), (wq_hbm, wq_ref), (wk_hbm, wk_ref), (wv_hbm, wv_ref)]
+        )
+    ]
+    for each in local:
+        each.start()
+    greet(
+        xs + zs + [near, across, beside, sibling]
+        + [device(group_at(*o), half, spot, core) for o in offsets[3:]]
+    )
 
     def copy(src, dst, send, recv, to):
         return pltpu.make_async_remote_copy(
@@ -366,8 +416,8 @@
     def y_start(j):
         part = pl.ds(pl.multiple_of((theirs_first + j) * quarter, quarter), quarter)
         sources = [
-            wq_ref.at[part, pl.ds(0, HEAD)], wq_ref.at[part, pl.ds(HEAD, HEAD)],
-            wk_ref.at[part], wv_ref.at[part],
+            wq_hbm.at[part, pl.ds(0, HEAD)], wq_hbm.at[part, pl.ds(HEAD, HEAD)],
+            wk_hbm.at[part], wv_hbm.at[part],
         ]
         for z, src in enumerate(sources):
             @pl.when(depth == z)
@@ -397,12 +447,50 @@
         part = pl.ds(pl.multiple_of(q * out_quarter + n * size, size), size)
         return copy(src.at[part], wo_across_ref.at[part], o_send.at[i], o_recv.at[i], to)
 
+    pages, stretch = ck_ref.shape[:2]
+    groups = table_ref.shape[0]
+
+    def picked(target):
+        index = 0
+        for c in range(table_ref.shape[1]):
+            page = table_ref[target, c]
+            index = index + jnp.where(page // pages == group, page % pages, 0)
+        return index
+
+    def p_copy(j, source):
+        return copy(
+            outgoing.at[j], pages_ref.at[source], p_send.at[j], p_recv.at[j],
+            device(group_at(*offsets[j]), half, spot, core),
+        )
+
+    def send_pages():
+        for each in local[:2]:
+            each.wait()
+        for j, offset in enumerate(offsets):
+            index = picked(group_at(*offset))
+            outgoing[j, :, :HEAD] = ck_ref[index]
+            outgoing[j, :, HEAD:] = cv_ref[index]
+            p_copy(j, group).start()
+        index = picked(group)
+        pages_ref[group, :, :HEAD] = ck_ref[index]
+        pages_ref[group, :, HEAD:] = cv_ref[index]
+
+    def make_tables():
+        layout = Layout(owners_ref, counts_ref, stretch)
+        below = lax.broadcasted_iota(jnp.int32, (stretch, 1), 0)
+        for i in range(cos_ref.shape[0] // stretch):
+            row = below + (half * cos_ref.shape[0] + i * stretch)
+            code = layout.of_queries(row - selected)
+            if i == 0:
+                code = jnp.where(row < selected, layout.of_cached(ids_ref[...]), code)
+            angle = (code - request_base(code)).astype(jnp.float32) * freq_ref[...]
+            sine = jnp.sin(angle)
+            lane = lax.broadcasted_iota(jnp.int32, sine.shape, 1)
+            cos_ref[pl.ds(i * stretch, stretch), :] = jnp.cos(angle)
+            sin_ref[pl.ds(i * stretch, stretch), :] = jnp.where(lane < HEAD // 2, -sine, sine)
+
     def table(ref, owner):
-        start = pl.multiple_of((half * AROUND + owner) * 2 * rows, 2 * rows)
-        return ref[pl.ds(start, 2 * rows), :]
-
-    def turned(u, cosine, sine):
-        return u * cosine + pltpu.roll(u, HEAD // 2, 1) * sine
+        return ref[pl.ds(pl.multiple_of(owner * 2 * rows, 2 * rows), 2 * rows), :]
 
     def own_heads(owner):
         source = normed[owner]
@@ -460,6 +548,10 @@
     x_copy(0).start()
     x_copy(1).start()
     s_copy(0, spot).start()
+    send_pages()
+    make_tables()
+    for each in local[2:]:
+        each.wait()
     for n in range(2):
         y_done(n).wait_recv()
         w_copy(n, depth, mine_first + n).start()
@@ -540,32 +632,52 @@
         y_done(n).wait_send()
     for i in range(8):
         o_copy(i, wo_across_ref, depth, 0, near).wait_send()
-
-
-def project_in(own_rows, gain, w_query, w_key, w_value, cosine, sine, w_out):
+    for j, (low, deep) in enumerate(offsets):
+        p_copy(j, group_at(low, -deep)).wait()
+
+
+def project_in(
+    own_rows, gain, w_query, w_key, w_value, w_out, cache_keys, cache_values,
+    owners, counts, table, selected, ids_col, new_rows,
+):
     rows, features = own_rows.shape
+    pages, stretch = cache_keys.shape[:2]
     vmem = pl.BlockSpec(memory_space=pltpu.VMEM)
+    smem = pl.BlockSpec(memory_space=pltpu.SMEM)
     hbm = pl.BlockSpec(memory_space=pl.ANY)
     dma = pltpu.SemaphoreType.DMA
-    pairs = [(2,), (2,), (4,), (2,), (4,), (2, 4), (2,), (8,), (4, 4)]
+    pairs = [(7,), (2,), (2,), (4,), (2,), (4,), (2, 4), (2,), (8,), (4, 4)]
+    bf16 = jnp.bfloat16
     return pl.pallas_call(
-        project_in_kernel,
+        functools.partial(project_in_kernel, selected),
         out_shape=(
-            jax.ShapeDtypeStruct((4, cosine.shape[0], HEAD), jnp.bfloat16),
-            jax.ShapeDtypeStruct(w_out.shape, jnp.bfloat16),
+            jax.ShapeDtypeStruct((4, new_rows, HEAD), bf16),
+            jax.ShapeDtypeStruct(w_out.shape, bf16),
+            jax.ShapeDtypeStruct((table.shape[0], stretch, 2 * HEAD), bf16),
         ),
-        in_specs=[vmem] * 7 + [hbm],
-        out_specs=(vmem, hbm),
+        in_specs=[smem] * 3 + [vmem] * 4 + [hbm] * 6,
+        out_specs=(vmem, hbm, vmem),
         scratch_shapes=[
-            pltpu.VMEM((AROUND, 2 * rows, features), jnp.bfloat16),
-            pltpu.VMEM((4, features, HEAD), jnp.bfloat16),
-            pltpu.VMEM((4, 4, 2 * rows, HEAD), jnp.bfloat16),
+            pltpu.VMEM((AROUND, 2 * rows, features), bf16),
+            pltpu.VMEM((4, features, HEAD), bf16),
+            pltpu.VMEM((4, 4, 2 * rows, HEAD), bf16),
+            pltpu.VMEM(w_query.shape, bf16), pltpu.VMEM(w_key.shape, bf16),
+            pltpu.VMEM(w_value.shape, bf16),
+            pltpu.VMEM(cache_keys.shape, bf16), pltpu.VMEM(cache_values.shape, bf16),
+            pltpu.VMEM((7, stretch, 2 * HEAD), bf16),
+            pltpu.VMEM((new_rows // 2, HEAD), jnp.float32),
+            pltpu.VMEM((new_rows // 2, HEAD), jnp.float32),
+            dma((5,)),
         ] + [dma(shape) for shape in pairs for _ in range(2)],
         compiler_params=pltpu.CompilerParams(
-            collective_id=2, has_side_effects=True, vmem_limit_bytes=48 << 20
+            collective_id=2, has_side_effects=True, vmem_limit_bytes=52 << 20
         ),
         name="project_in",
-    )(own_rows, gain[None, :], w_query, w_key, w_value, cosine, sine, w_out)
+    )(
+        owners, counts, table, own_rows, gain[None, :],
+        np.concatenate([frequencies()] * 2)[None, :], ids_col,
+        w_query, w_key, w_value, cache_keys, cache_values, w_out,
+    )
 
 
 def on_device(
@@ -573,33 +685,18 @@
     page_table, stretch_request, recompute_ids, query_counts,
 ):
     own_rows = hidden[0]
-    tok_total = lax.axis_size("tok")
-    groups = lax.axis_size("grp")
-    new_rows = own_rows.shape[0] * tok_total
-    pages, stretch_len = cache_keys.shape[:2]
-    group = lax.axis_index("grp")
-    mine = page_table // pages == group
-    local = jnp.sum(jnp.where(mine, page_table % pages, 0), axis=1)
-    picks = (local[:, None] == jnp.arange(pages, dtype=jnp.int32)[None, :]).astype(jnp.bfloat16)
-    both = jnp.concatenate([cache_keys, cache_values], axis=-1)
-    send = jnp.einsum("gp,pkh->gkh", picks, both, preferred_element_type=jnp.float32).astype(
-        jnp.bfloat16
+    new_rows = own_rows.shape[0] * lax.axis_size("tok")
+    stretch = cache_keys.shape[1]
+    owners, counts, ids = stretch_request[0], query_counts[0], recompute_ids[0]
+    selected = ids.shape[0]
+    padded = jnp.pad(ids, (0, stretch - selected), constant_values=-1)
+    ids_col, ids_row = padded[:, None], padded[None, :]
+    heads, w_across, pages = project_in(
+        own_rows, input_gain, w_query, w_key, w_value, w_out, cache_keys, cache_values,
+        owners, counts, page_table, selected, ids_col, new_rows,
     )
-    got = lax.all_to_all(send, "grp", 0, 0, tiled=True)
-    got = got.reshape(groups * stretch_len, 2 * HEAD)
-    table_row = lax.dynamic_index_in_dim(page_table, group, 0, keepdims=False)
-    shift_of, row_req, row_pos, row_code, key_code, live = request_layout(
-        stretch_request[0], query_counts[0], recompute_ids[0], table_row, (groups, pages),
-        stretch_len, new_rows,
-    )
-    pcos, psin = angles_of(shift_of)
-    cosine, sine = angles_of(row_pos)
-    heads, w_across = project_in(own_rows, input_gain, w_query, w_key, w_value, cosine, sine, w_out)
-    attended = attention(
-        heads, got[:, :HEAD], got[:, HEAD:], pcos, psin, row_code, key_code, live
-    )
-    output = project(attended, w_out, w_across, own_rows, post_gain)
-    return output[None]
+    attended = attention(heads, pages, owners, counts, page_table, selected, ids_col, ids_row)
+    return project(attended, w_out, w_across, own_rows, post_gain)[None]
 
 
 def solution(mesh):

time: 204 us -> 182 us (0.89)
  other arithmetic: 7.95 us -> 0 us
  starting transfers between devices: 6.87 us -> 0 us
  Pallas kernels: 172 us -> 168 us
  local copies, waits for them, and re-layouts: 15.7 us -> 13 us
    all_to_all x1 -> x0, starting transfers between devices: 6.87 us -> none  [on_device(): got = lax.all_to_all(send, 'grp', 0, 0, tiled=True)]
    neg x2 -> x0, other arithmetic: 3.84 us -> none  [angles_of(): -sine]
    pallas_call x2, Pallas kernels: 111 us -> 109 us  [the longest x1 89.4 us: project_in(): pl.pallas_call(functools.partial(project_in_kernel, selected), out_shape=...]
    concatenate x3 -> x0, other arithmetic: 2.1 us -> none  [the longest x2 2.02 us: angles_of(): jnp.concatenate([cosine, cosine], axis=1)]
    unnamed x31 -> x25, local copies, waits for them, and re-layouts: 11.6 us -> 10.9 us
  transfers between devices with their start and end apart: 1 -> 0, of which waited for: 0 -> 0; matrix products, arithmetic and copies ran while one was open for 5% -> 0% of each run, Pallas kernels for 40% -> 0%
where the time goes in v1:
time: 182 us; the launch traced here: 181 us
  Pallas kernels  168 us (92%)
  local copies, waits for them, and re-layouts  13 us (7%)
    pallas_call x1, Pallas kernels, project_in(): pl.pallas_call(functools.partial(project_in_kernel, selected), out_shape=...  89.4 us
    pallas_call x1, Pallas kernels, project(): pl.pallas_call(project_kernel, out_shape=jax.ShapeDtypeStruct((rows, feat...  58.9 us
    pallas_call x1, Pallas kernels, attention(): pl.pallas_call(functools.partial(attention_kernel, selected), out_shape=j...  19.8 us
    unnamed x25, local copies, waits for them, and re-layouts  10.9 us

profile of v1, /device:TPU:1, one launch (start us, length us, event | category | flops | bytes accessed | tf_op | source)
XLA Modules:
  0.0 181.3 jit_solution(3226727555203816696)
XLA Ops:
  0.0 0.7 pad.4
  0.7 0.1 copy.17.ids_ref.ids_col_ref
  0.8 0.7 broadcast_in_dim.15.gain_ref
  1.6 0.0 copy-start.3
  1.6 1.0 copy-done.3
  2.6 0.0 copy-start.4
  2.6 1.0 copy-done.4
  3.7 0.0 copy-start.5
  3.7 0.7 copy-done.5
  4.3 0.0 copy-start.8
  4.4 0.7 copy-done.8
  5.0 0.0 copy-start.9
  5.0 0.7 copy-done.9
  5.7 0.0 copy-start.10
  5.7 0.7 copy-done.10
  6.3 0.0 copy-start.6
  6.3 0.0 copy-start.7
  6.3 89.4 %project_in.1 = (bf16[4,2048,128]{2,1,0:T(8,128)(2,1)}, bf16[256,4608]{1,0:T(8,128)(2,1)}, bf16[8,256,256]{2,1,0:T(8,128)(2,1)}) custom-call(s32[8]{0:T(128)S(1)} %bitcast.9, s32[3]{0:T(128)S(1)} %bitcast.11, s32[8,8]{1,0:T(8,128)S(1)} %copy-done.5, bf16[128,4608]{1,0:T(8,128)(2,1)} %bitcast.14, f32[1,4608]{1,0:T(1,128)S(1)} %broadcast_in_dim.15.gain_ref, ...), custom_call_target="tpu_custom_call" | custom-call | tf_op jit(solution)/shard_map/project_in/pallas_call | solution.py:651
  95.7 0.0 copy-done.6
  95.7 0.0 copy-done.7
  95.8 0.0 copy-start.1
  95.8 1.6 copy-done.1
  97.3 0.0 copy-start.2
  97.4 1.2 copy-done.2
  98.6 0.0 copy-start.11
  98.6 19.8 %attention.1.attn_ref = bf16[2048,256]{1,0:T(8,128)(2,1)S(1)} custom-call(s32[8]{0:T(128)S(1)} %bitcast.10, s32[3]{0:T(128)S(1)} %bitcast.12, s32[8,8]{1,0:T(8,128)S(1)} %copy-done.5, bf16[4,2048,128]{2,1,0:T(8,128)(2,1)S(1)} %copy-done.1, bf16[8,256,256]{2,1,0:T(8,128)(2,1)S(1)} %copy-done.2, f32[8,128]{1,0:T(8,128)S(1)} %copy-done.7, ...), custom_call_target="tpu_custom_call" | custom-call | tf_op jit(solution)/shard_map/attention/pallas_call | solution.py:165
  118.4 0.0 copy-start
  118.4 1.0 copy-done
  119.4 0.0 copy-done.11
  119.4 0.6 broadcast_in_dim.18.gain_ref
  120.0 58.9 %project.1 = bf16[128,4608]{1,0:T(8,128)(2,1)} custom-call(bf16[2048,256]{1,0:T(8,128)(2,1)} %copy-done, bf16[256,4608]{1,0:T(8,128)(2,1)} %w0_ref.1, bf16[256,4608]{1,0:T(8,128)(2,1)} %get-tuple-element.10.w1_ref, bf16[128,4608]{1,0:T(8,128)(2,1)} %bitcast.15, f32[1,4608]{1,0:T(1,128)} %broadcast_in_dim.18.gain_ref), custom_call_target="tpu_custom_call" | custom-call | tf_op jit(solution)/shard_map/project/pallas_call | solution.py:321
  178.9 2.4 %copy.20 = bf16[1,128,4608]{2,1,0:T(8,128)(2,1)} copy(bf16[1,128,4608]{2,1,0:T(8,128)(2,1)} %bitcast.13) | data formatting | bytes 2359296
Async XLA Ops:
  1.6 1.0 copy-start.3
  2.6 1.0 copy-start.4
  3.7 0.7 copy-start.5
  4.3 0.7 copy-start.8
  5.0 0.7 copy-start.9
  5.7 0.7 copy-start.10
  6.3 89.4 %copy-start.6 = (f32[8,128]{1,0:T(8,128)S(1)}, f32[8,128]{1,0:T(8,128)}, u32[]{:S(2)}) copy-start(f32[8,128]{1,0:T(8,128)} %constant.10.clone.psin_ref) | copy-start | bytes 12292
  6.3 89.4 %copy-start.7 = (f32[8,128]{1,0:T(8,128)S(1)}, f32[8,128]{1,0:T(8,128)}, u32[]{:S(2)}) copy-start(f32[8,128]{1,0:T(8,128)} %constant.9.clone.pcos_ref) | copy-start | bytes 12292
  95.8 1.6 copy-start.1
  97.3 1.2 copy-start.2
  98.6 20.8 %copy-start.11 = (f32[4608]{0:T(1024)S(1)}, f32[4608]{0:T(1024)}, u32[]{:S(2)}) copy-start(f32[4608]{0:T(1024)} %param.22) | copy-start | bytes 55300
  118.4 1.0 copy-start

commit v2 on v1

--- a/solution.py
+++ b/solution.py
@@ -65,9 +65,30 @@
         return (m >= self.starts[1]).astype(jnp.int32) + (m >= self.starts[2]).astype(jnp.int32)
 
 
-def attention_kernel(
+MESH = pl.DeviceIdType.MESH
+RINGS = 4
+AROUND = 4
+
+
+def place():
+    tok = lax.axis_index("tok")
+    return lax.axis_index("grp"), tok // 8, (tok // 2) % AROUND, tok % 2
+
+
+def device(group, half, spot, core):
+    return (group, half * 8 + lax.rem(spot + 2 * AROUND, AROUND) * 2 + core)
+
+
+def greet(partners):
+    barrier = pltpu.get_barrier_semaphore()
+    for partner in partners:
+        pl.semaphore_signal(barrier, inc=1, device_id=partner, device_id_type=MESH)
+    pl.semaphore_wait(barrier, len(partners))
+
+
+def make_attention(
     selected, owners_ref, counts_ref, table_ref, heads_ref, pages_ref, pcos_ref, psin_ref,
-    ids_col_ref, ids_row_ref, out_ref, keys, values, key_codes, row_codes, row_bases, queries, total,
+    ids_col_ref, ids_row_ref, attended, keys, values, key_codes, row_codes, row_bases, queries, total,
 ):
     rows = heads_ref.shape[1]
     groups, stretch = pages_ref.shape[:2]
@@ -109,17 +130,15 @@
 
     ahead = cached // BLOCK
 
-    def row_block(rb, carry):
+    def row_block(rb):
         here = pl.ds(pl.multiple_of(rb * BLOCK, BLOCK), BLOCK)
         queries[:BLOCK, :] = heads_ref[0, here, :]
         queries[BLOCK:, :] = heads_ref[1, here, :]
         total[...] = jnp.zeros_like(total)
         code = row_codes[here, :]
         base = row_bases[here, :]
-        low = jnp.where(rb == 0, 0, layout.request_of(rb * BLOCK - selected))
-        high = jnp.where(rb == 0, 2, layout.request_of(rb * BLOCK - selected + BLOCK - 1))
-
-        def attend(kb):
+
+        def key_block(kb, carry):
             there = pl.ds(pl.multiple_of(kb * BLOCK, BLOCK), BLOCK)
             scores = lax.dot_general(
                 queries[...], keys[there, :], (((1,), (1,)), ((), ())),
@@ -132,84 +151,21 @@
             both = jnp.concatenate([seen, seen], axis=0)
             rounded = jnp.where(both, weights, 0.0).astype(jnp.bfloat16)
             total[...] += jnp.dot(rounded, values[there, :], preferred_element_type=jnp.float32)
-
-        def key_block(kb, inner_carry):
-            slot = jnp.minimum(kb * per, groups - per)
-            from_cache = (owners_ref[slot] <= high) & (owners_ref[slot + per - 1] >= low)
-            last = (kb - ahead + 1) * BLOCK - 1 - selected
-            from_new = (kb == ahead) | (layout.request_of(last) >= low)
-
-            @pl.when(((kb < ahead) & from_cache) | ((kb >= ahead) & from_new))
-            def _():
-                attend(kb)
-
-            return inner_carry
+            return carry
 
         lax.fori_loop(0, ahead + rb + 1, key_block, 0)
-        result = total[:, :HEAD] / total[:, HEAD:]
-        out_ref[here, :HEAD] = result[:BLOCK].astype(jnp.bfloat16)
-        out_ref[here, HEAD:] = result[BLOCK:].astype(jnp.bfloat16)
-        return carry
-
-    lax.fori_loop(0, rows // BLOCK, row_block, 0)
-
-
-def attention(heads, pages, owners, counts, table, selected, ids_col, ids_row):
-    rows = heads.shape[1]
-    groups, stretch = pages.shape[:2]
-    total_keys = groups * stretch + rows
-    angles = (np.arange(groups, dtype=np.float32) * stretch)[:, None] * frequencies()[None, :]
-    cosine, sine = np.cos(angles), np.sin(angles)
-    vmem = pl.BlockSpec(memory_space=pltpu.VMEM)
-    smem = pl.BlockSpec(memory_space=pltpu.SMEM)
-    return pl.pallas_call(
-        functools.partial(attention_kernel, selected),
-        out_shape=jax.ShapeDtypeStruct((rows, 2 * HEAD), jnp.bfloat16),
-        in_specs=[smem] * 3 + [vmem] * 6,
-        out_specs=vmem,
-        scratch_shapes=[
-            pltpu.VMEM((total_keys, HEAD), jnp.bfloat16),
-            pltpu.VMEM((total_keys, 2 * HEAD), jnp.bfloat16),
-            pltpu.VMEM((total_keys // BLOCK, 1, BLOCK), jnp.int32),
-            pltpu.VMEM((rows, 1), jnp.int32),
-            pltpu.VMEM((rows, 1), jnp.int32),
-            pltpu.VMEM((2 * BLOCK, HEAD), jnp.bfloat16),
-            pltpu.VMEM((2 * BLOCK, 2 * HEAD), jnp.float32),
-        ],
-        compiler_params=pltpu.CompilerParams(vmem_limit_bytes=40 << 20),
-        name="attention",
-    )(
-        owners, counts, table, heads, pages,
-        np.concatenate([cosine, cosine], axis=1), np.concatenate([-sine, sine], axis=1),
-        ids_col, ids_row,
-    )
-
-
-MESH = pl.DeviceIdType.MESH
-RINGS = 4
-AROUND = 4
-
-
-def place():
-    tok = lax.axis_index("tok")
-    return lax.axis_index("grp"), tok // 8, (tok // 2) % AROUND, tok % 2
-
-
-def device(group, half, spot, core):
-    return (group, half * 8 + lax.rem(spot + 2 * AROUND, AROUND) * 2 + core)
-
-
-def greet(partners):
-    barrier = pltpu.get_barrier_semaphore()
-    for partner in partners:
-        pl.semaphore_signal(barrier, inc=1, device_id=partner, device_id_type=MESH)
-    pl.semaphore_wait(barrier, len(partners))
+        quotient = total[:, :HEAD] / total[:, HEAD:]
+        attended[here, :HEAD] = quotient[:BLOCK].astype(jnp.bfloat16)
+        attended[here, HEAD:] = quotient[BLOCK:].astype(jnp.bfloat16)
+
+    return row_block
 
 
 def project_kernel(
-    attn_ref, w0_ref, w1_ref, hid_ref, gain_ref, out_ref,
-    other, product, own, pair_out, pair_in, ring_out, ring_in, result,
-    other_send, other_recv, pair_send, pair_recv, ring_send, ring_recv,
+    selected, owners_ref, counts_ref, table_ref, heads_ref, pages_ref, pcos_ref, psin_ref,
+    ids_col_ref, ids_row_ref, w0_ref, hid_ref, gain_ref, out_ref,
+    attn_ref, keys, values, key_codes, row_codes, row_bases, queries, total, w1_ref, other, product, own, pair_out, pair_in, ring_out, ring_in, result,
+    other_send, other_recv, pair_send, pair_recv, ring_send, ring_recv, o_send, o_recv,
 ):
     group, half, spot, core = place()
     rows = hid_ref.shape[0]
@@ -217,7 +173,34 @@
     chunk = 2 * rows
     across = device(group, 1 - half, spot, core)
     sibling = device(group, half, spot, 1 - core)
-    greet([across, sibling, device(group, half, spot + 1, core), device(group, half, spot - 1, core)])
+    lows, depth = group // AROUND, group % AROUND
+    zs = [
+        device(lows * AROUND + lax.rem(depth + 1, AROUND), half, spot, core),
+        device(lows * AROUND + lax.rem(depth + AROUND - 1, AROUND), half, spot, core),
+    ]
+    near = device((1 - lows) * AROUND + depth, 1 - half, spot, core)
+    beside = device((1 - lows) * AROUND + depth, half, spot, core)
+    greet(
+        [across, sibling, device(group, half, spot + 1, core), device(group, half, spot - 1, core)]
+        + zs + [near, beside]
+    )
+
+    def o_copy(i, src, step, n, to):
+        size = w0_ref.shape[0] // (2 * AROUND)
+        piece = lax.rem(depth + step + AROUND, AROUND) * 2 + n
+        part = pl.ds(pl.multiple_of(piece * size, size), size)
+        return pltpu.make_async_remote_copy(
+            src_ref=src.at[part], dst_ref=w1_ref.at[part], send_sem=o_send.at[i],
+            recv_sem=o_recv.at[i], device_id=to, device_id_type=MESH,
+        )
+
+    first, second = lows, 1 - lows
+    o_copy(0, w0_ref, 0, second, near).start()
+    row_block = make_attention(
+        selected, owners_ref, counts_ref, table_ref, heads_ref, pages_ref, pcos_ref, psin_ref,
+        ids_col_ref, ids_row_ref, attn_ref, keys, values, key_codes, row_codes, row_bases, queries,
+        total,
+    )
 
     def other_copy(j):
         owner = lax.rem(spot + (3, 1, 2, 0)[j], AROUND)
@@ -242,8 +225,36 @@
             device_id=device(group, half, spot + 1 - 2 * (r // 2), core), device_id_type=MESH,
         )
 
+    per_half = attn_ref.shape[0] // BLOCK // 2
+
+    def attend(base_half, first_block):
+        def step(i, carry):
+            row_block(base_half * per_half + i)
+            return carry
+
+        lax.fori_loop(first_block, first_block + 1, step, 0)
+
+    attend(1 - half, 0)
+    o_copy(0, w1_ref, 0, first, near).wait_recv()
+    o_copy(1, w1_ref, 0, first, beside).start()
+    for d in range(2):
+        o_copy(2 + d, w1_ref, 0, first, zs[d]).start()
+    attend(1 - half, 1)
     for j in range(4):
         other_copy(j).start()
+    o_copy(1, w1_ref, 0, second, beside).wait_recv()
+    for d in range(2):
+        o_copy(4 + d, w1_ref, 0, second, zs[d]).start()
+    o_copy(2, w1_ref, -1, first, zs[0]).wait_recv()
+    o_copy(6, w1_ref, -1, first, zs[0]).start()
+    attend(half, 0)
+    o_copy(5, w1_ref, 1, second, zs[1]).wait_recv()
+    o_copy(7, w1_ref, 1, second, zs[1]).start()
+    attend(half, 1)
+    o_copy(3, w1_ref, 1, first, zs[1]).wait_recv()
+    o_copy(4, w1_ref, -1, second, zs[0]).wait_recv()
+    o_copy(6, w1_ref, 2, first, zs[0]).wait_recv()
+    o_copy(7, w1_ref, 2, second, zs[1]).wait_recv()
 
     def partial(s, r):
         owner = lax.rem(spot + (2 * (r // 2) - 1) * (1 + s) + 2 * AROUND, AROUND)
@@ -297,6 +308,8 @@
     forward(3)
     for j in range(4):
         other_copy(j).wait_send()
+    for i in range(8):
+        o_copy(i, w1_ref, 0, first, near).wait_send()
 
     def drain(r, carry):
         for s in range(4):
@@ -313,18 +326,33 @@
     ).astype(jnp.bfloat16)
 
 
-def project(attended, w_own, w_across, own_rows, post_gain):
+def project(heads, pages, owners, counts, table, selected, ids_col, ids_row, w_own, own_rows, post_gain):
     rows, features = own_rows.shape
     width = features // RINGS
+    new_rows = heads.shape[1]
+    groups, stretch = pages.shape[:2]
+    total_keys = groups * stretch + new_rows
+    angles = (np.arange(groups, dtype=np.float32) * stretch)[:, None] * frequencies()[None, :]
+    cosine, sine = np.cos(angles), np.sin(angles)
     vmem = pl.BlockSpec(memory_space=pltpu.VMEM)
+    smem = pl.BlockSpec(memory_space=pltpu.SMEM)
     dma = pltpu.SemaphoreType.DMA
     return pl.pallas_call(
-        project_kernel,
+        functools.partial(project_kernel, selected),
         out_shape=jax.ShapeDtypeStruct((rows, features), jnp.bfloat16),
-        in_specs=[vmem] * 5,
+        in_specs=[smem] * 3 + [vmem] * 9,
         out_specs=vmem,
         scratch_shapes=[
-            pltpu.VMEM((4, 2 * rows, attended.shape[1]), jnp.bfloat16),
+            pltpu.VMEM((new_rows, 2 * HEAD), jnp.bfloat16),
+            pltpu.VMEM((total_keys, HEAD), jnp.bfloat16),
+            pltpu.VMEM((total_keys, 2 * HEAD), jnp.bfloat16),
+            pltpu.VMEM((total_keys // BLOCK, 1, BLOCK), jnp.int32),
+            pltpu.VMEM((new_rows, 1), jnp.int32),
+            pltpu.VMEM((new_rows, 1), jnp.int32),
+            pltpu.VMEM((2 * BLOCK, HEAD), jnp.bfloat16),
+            pltpu.VMEM((2 * BLOCK, 2 * HEAD), jnp.float32),
+            pltpu.VMEM(w_own.shape, jnp.bfloat16),
+            pltpu.VMEM((4, 2 * rows, 2 * HEAD), jnp.bfloat16),
             pltpu.VMEM((2 * rows, width), jnp.float32),
             pltpu.VMEM((4, RINGS, rows, width), jnp.float32),
             pltpu.VMEM((4, RINGS, rows, width), jnp.bfloat16),
@@ -333,28 +361,32 @@
             pltpu.VMEM((3, RINGS, rows, width), jnp.bfloat16),
             pltpu.VMEM((rows, features), jnp.float32),
             dma((4,)), dma((4,)), dma((4, RINGS)), dma((4, RINGS)), dma((3, RINGS)), dma((3, RINGS)),
+            dma((8,)), dma((8,)),
         ],
         compiler_params=pltpu.CompilerParams(
-            collective_id=1, has_side_effects=True, vmem_limit_bytes=56 << 20
+            collective_id=1, has_side_effects=True, vmem_limit_bytes=60 << 20
         ),
         name="project",
-    )(attended, w_own, w_across, own_rows, post_gain[None, :])
+    )(
+        owners, counts, table, heads, pages,
+        np.concatenate([cosine, cosine], axis=1), np.concatenate([-sine, sine], axis=1),
+        ids_col, ids_row, w_own, own_rows, post_gain[None, :],
+    )
 
 
 def project_in_kernel(
     selected, owners_ref, counts_ref, table_ref, hid_ref, gain_ref, freq_ref, ids_ref,
-    wq_hbm, wk_hbm, wv_hbm, ck_hbm, cv_hbm, wo_ref,
-    heads_ref, wo_across_ref, pages_ref,
+    wq_hbm, wk_hbm, wv_hbm, ck_hbm, cv_hbm,
+    heads_ref, pages_ref,
     normed, weights, ship, wq_ref, wk_ref, wv_ref, ck_ref, cv_ref, outgoing, cos_ref, sin_ref,
     l_sem, p_send, p_recv, x_send, x_recv, f_send, f_recv, s_send, s_recv, y_send, y_recv, w_send, w_recv, z_send, z_recv,
-    g_send, g_recv, o_send, o_recv, e_send, e_recv,
+    g_send, g_recv, e_send, e_recv,
 ):
     group, half, spot, core = place()
     rows, features = hid_ref.shape
     depth = group % AROUND
     lows = group // AROUND
     quarter = features // 4
-    out_quarter = wo_ref.shape[0] // 4
 
     def around(value):
         return lax.rem(value + 2 * AROUND, AROUND)
@@ -414,7 +446,8 @@
         return weights.at[q, pl.ds(pl.multiple_of(p * quarter, quarter), quarter)]
 
     def y_start(j):
-        part = pl.ds(pl.multiple_of((theirs_first + j) * quarter, quarter), quarter)
+        piece = (theirs_first if j < 2 else mine_first) + j % 2
+        part = pl.ds(pl.multiple_of(piece * quarter, quarter), quarter)
         sources = [
             wq_hbm.at[part, pl.ds(0, HEAD)], wq_hbm.at[part, pl.ds(HEAD, HEAD)],
             wk_hbm.at[part], wv_hbm.at[part],
@@ -422,10 +455,10 @@
         for z, src in enumerate(sources):
             @pl.when(depth == z)
             def _(src=src):
-                copy(src, slab(depth, theirs_first + j), y_send.at[j], y_recv.at[j], near).start()
+                copy(src, slab(depth, piece), y_send.at[j], y_recv.at[j], near).start()
 
     def y_done(j):
-        piece = slab(depth, mine_first + j)
+        piece = slab(depth, nth_piece(j))
         return copy(piece, piece, y_send.at[j], y_recv.at[j], near)
 
     def w_copy(i, q, p):
@@ -441,11 +474,6 @@
     def g_copy(d, q):
         piece = slab(q, mine_first + d)
         return copy(piece, piece, g_send.at[d], g_recv.at[d], zs[d])
-
-    def o_copy(i, src, q, n, to):
-        size = out_quarter // 2
-        part = pl.ds(pl.multiple_of(q * out_quarter + n * size, size), size)
-        return copy(src.at[part], wo_across_ref.at[part], o_send.at[i], o_recv.at[i], to)
 
     pages, stretch = ck_ref.shape[:2]
     groups = table_ref.shape[0]
@@ -554,14 +582,13 @@
         each.wait()
     for n in range(2):
         y_done(n).wait_recv()
-        w_copy(n, depth, mine_first + n).start()
         z_copy(0, n).start()
         z_copy(1, n).start()
-    o_copy(0, wo_ref, depth, 1 - lows, near).start()
+        y_start(n + 2)
     s_copy(0, spot, twin).wait_recv()
     own_blocks(0, 1)
     for n in range(2):
-        w_copy(n, depth, theirs_first + n).wait_recv()
+        y_done(n + 2).wait_recv()
         z_copy(0, n + 2).start()
         z_copy(1, n + 2).start()
     their_blocks(0, 1, 0, 1)
@@ -569,8 +596,6 @@
     g_copy(0, below).start()
     z_copy(1, 1, above).wait_recv()
     g_copy(1, above).start()
-    o_copy(0, wo_ref, depth, lows, near).wait_recv()
-    o_copy(1, wo_across_ref, depth, lows, beside).start()
     x_copy(0, left).wait_recv()
     f_copy(0, left).start()
     s_copy(1, left).start()
@@ -585,32 +610,20 @@
     for n in (0, 2, 3):
         z_copy(1, n, above).wait_recv()
     g_copy(0, beyond).wait_recv()
-    w_copy(2, beyond, mine_first).start()
+    w_copy(0, beyond, mine_first).start()
     g_copy(1, beyond).wait_recv()
-    w_copy(3, beyond, mine_first + 1).start()
-    o_copy(1, wo_across_ref, depth, 1 - lows, beside).wait_recv()
-    for n in range(2):
-        o_copy(2 + n, wo_across_ref, depth, n, zs[0]).start()
-        o_copy(4 + n, wo_across_ref, depth, n, zs[1]).start()
+    w_copy(1, beyond, mine_first + 1).start()
     their_blocks(1, 3, 0, 3)
     own_blocks(1, 3)
-    w_copy(2, beyond, theirs_first).wait_recv()
-    w_copy(3, beyond, theirs_first + 1).wait_recv()
+    w_copy(0, beyond, theirs_first).wait_recv()
+    w_copy(1, beyond, theirs_first + 1).wait_recv()
     their_blocks(3, 4, 0, 3)
     f_copy(0, far).wait_recv()
     f_copy(1, far).wait_recv()
     s_copy(3, far).start()
     s_copy(3, far, twin).wait_recv()
     their_blocks(0, 4, 3, 4)
-    o_copy(2, wo_across_ref, below, 0, zs[0]).wait_recv()
-    o_copy(6, wo_across_ref, below, 0, zs[0]).start()
-    o_copy(5, wo_across_ref, above, 1, zs[1]).wait_recv()
-    o_copy(7, wo_across_ref, above, 1, zs[1]).start()
     own_blocks(3, 4)
-    o_copy(3, wo_across_ref, below, 1, zs[0]).wait_recv()
-    o_copy(4, wo_across_ref, above, 0, zs[1]).wait_recv()
-    o_copy(6, wo_across_ref, beyond, 0, zs[0]).wait_recv()
-    o_copy(7, wo_across_ref, beyond, 1, zs[1]).wait_recv()
     for i in range(4):
         for b in range(4):
             to = pl.ds(
@@ -627,36 +640,34 @@
         g_copy(d, quarters[1 + d]).wait_send()
     for i in range(4):
         s_copy(i, owners[i]).wait_send()
-        w_copy(i, (depth, depth, beyond, beyond)[i], mine_first + i % 2).wait_send()
     for n in range(2):
+        w_copy(n, beyond, mine_first + n).wait_send()
+    for n in range(4):
         y_done(n).wait_send()
-    for i in range(8):
-        o_copy(i, wo_across_ref, depth, 0, near).wait_send()
     for j, (low, deep) in enumerate(offsets):
         p_copy(j, group_at(low, -deep)).wait()
 
 
 def project_in(
-    own_rows, gain, w_query, w_key, w_value, w_out, cache_keys, cache_values,
+    own_rows, gain, w_query, w_key, w_value, cache_keys, cache_values,
     owners, counts, table, selected, ids_col, new_rows,
 ):
     rows, features = own_rows.shape
     pages, stretch = cache_keys.shape[:2]
     vmem = pl.BlockSpec(memory_space=pltpu.VMEM)
     smem = pl.BlockSpec(memory_space=pltpu.SMEM)
-    hbm = pl.BlockSpec(memory_space=pl.ANY)
+    hbm = pl.BlockSpec(memory_space=pltpu.HBM)
     dma = pltpu.SemaphoreType.DMA
-    pairs = [(7,), (2,), (2,), (4,), (2,), (4,), (2, 4), (2,), (8,), (4, 4)]
+    pairs = [(7,), (2,), (2,), (4,), (4,), (2,), (2, 4), (2,), (4, 4)]
     bf16 = jnp.bfloat16
     return pl.pallas_call(
         functools.partial(project_in_kernel, selected),
         out_shape=(
             jax.ShapeDtypeStruct((4, new_rows, HEAD), bf16),
-            jax.ShapeDtypeStruct(w_out.shape, bf16),
             jax.ShapeDtypeStruct((table.shape[0], stretch, 2 * HEAD), bf16),
         ),
-        in_specs=[smem] * 3 + [vmem] * 4 + [hbm] * 6,
-        out_specs=(vmem, hbm, vmem),
+        in_specs=[smem] * 3 + [vmem] * 4 + [hbm] * 5,
+        out_specs=(vmem, vmem),
         scratch_shapes=[
             pltpu.VMEM((AROUND, 2 * rows, features), bf16),
             pltpu.VMEM((4, features, HEAD), bf16),
@@ -676,7 +687,7 @@
     )(
         owners, counts, table, own_rows, gain[None, :],
         np.concatenate([frequencies()] * 2)[None, :], ids_col,
-        w_query, w_key, w_value, cache_keys, cache_values, w_out,
+        w_query, w_key, w_value, cache_keys, cache_values,
     )
 
 
@@ -691,12 +702,15 @@
     selected = ids.shape[0]
     padded = jnp.pad(ids, (0, stretch - selected), constant_values=-1)
     ids_col, ids_row = padded[:, None], padded[None, :]
-    heads, w_across, pages = project_in(
-        own_rows, input_gain, w_query, w_key, w_value, w_out, cache_keys, cache_values,
+    heads, pages = project_in(
+        own_rows, input_gain, w_query, w_key, w_value, cache_keys, cache_values,
         owners, counts, page_table, selected, ids_col, new_rows,
     )
-    attended = attention(heads, pages, owners, counts, page_table, selected, ids_col, ids_row)
-    return project(attended, w_out, w_across, own_rows, post_gain)[None]
+    output = project(
+        heads, pages, owners, counts, page_table, selected, ids_col, ids_row, w_out, own_rows,
+        post_gain,
+    )
+    return output[None]
 
 
 def solution(mesh):

time: 182 us -> 179 us (0.984)
  local copies, waits for them, and re-layouts: 13 us -> 9.99 us
    unnamed x25 -> x17, local copies, waits for them, and re-layouts: 10.9 us -> 7.1 us
    pallas_call x2 -> x1, Pallas kernels: 78.7 us -> 79.4 us  [project(): pl.pallas_call(functools.partial(project_kernel, selected), out_shape=jax...]
where the time goes in v2:
time: 179 us
  Pallas kernels  169 us (94%)
  local copies, waits for them, and re-layouts  9.99 us (6%)
    pallas_call x1, Pallas kernels, project_in(): pl.pallas_call(functools.partial(project_in_kernel, selected), out_shape=...  89.2 us
    pallas_call x1, Pallas kernels, project(): pl.pallas_call(functools.partial(project_kernel, selected), out_shape=jax...  79.4 us
    unnamed x17, local copies, waits for them, and re-layouts  7.1 us

profile of v2, /device:TPU:1, one launch (start us, length us, event | category | flops | bytes accessed | tf_op | source)
XLA Modules:
  0.0 178.6 jit_solution(15784809153300761123)
XLA Ops:
  0.0 0.7 pad.4
  0.7 0.0 copy-start.7
  0.7 0.7 broadcast_in_dim.15.gain_ref
  1.4 1.3 broadcast_in_dim.18.gain_ref
  2.8 0.1 copy.17.ids_ref.ids_col_ref
  2.9 0.0 copy-start.1
  2.9 1.0 copy-done.1
  4.0 0.0 copy-start.2
  4.0 1.0 copy-done.2
  5.0 0.0 copy-start.3
  5.0 0.7 copy-done.3
  5.7 0.0 copy-start.4
  5.7 0.7 copy-done.4
  6.3 0.0 copy-start.5
  6.3 0.7 copy-done.5
  7.0 0.0 copy-start.6
  7.0 0.7 copy-done.6
  7.7 0.0 copy-start
  7.7 89.2 %project_in.1 = (bf16[4,2048,128]{2,1,0:T(8,128)(2,1)}, bf16[8,256,256]{2,1,0:T(8,128)(2,1)}) custom-call(s32[8]{0:T(128)S(1)} %bitcast.8, s32[3]{0:T(128)S(1)} %bitcast.10, s32[8,8]{1,0:T(8,128)S(1)} %copy-done.3, bf16[128,4608]{1,0:T(8,128)(2,1)} %bitcast.12, f32[1,4608]{1,0:T(1,128)S(1)} %broadcast_in_dim.15.gain_ref, f32[1,128]{1,0:T(1,128)S(1)} %copy-done.6, ...), custom_call_target="tpu_custom_call" | custom-call | tf_op jit(solution)/shard_map/project_in/pallas_call | solution.py:663
  96.9 0.0 copy-done.7
  96.9 0.0 copy-done
  96.9 79.4 %project.1 = bf16[128,4608]{1,0:T(8,128)(2,1)} custom-call(s32[8]{0:T(128)} %bitcast.7, s32[3]{0:T(128)} %bitcast.9, s32[8,8]{1,0:T(8,128)} %table_ref.3, bf16[4,2048,128]{2,1,0:T(8,128)(2,1)} %get-tuple-element.7.heads_ref, bf16[8,256,256]{2,1,0:T(8,128)(2,1)} %get-tuple-element.8.pages_ref, f32[8,128]{1,0:T(8,128)} %constant.9.clone.pcos_ref, ...), custom_call_target="tpu_custom_call" | custom-call | tf_op jit(solution)/shard_map/project/pallas_call | solution.py:340
  176.3 2.4 %copy.20 = bf16[1,128,4608]{2,1,0:T(8,128)(2,1)} copy(bf16[1,128,4608]{2,1,0:T(8,128)(2,1)} %bitcast.11) | data formatting | bytes 2359296
Async XLA Ops:
  0.7 96.2 %copy-start.7 = (s32[256]{0:T(256)}, s32[256]{0:T(256)S(1)}, u32[]{:S(2)}) copy-start(s32[256]{0:T(256)S(1)} %pad.4) | copy-start | bytes 3076
  2.9 1.0 copy-start.1
  4.0 1.0 copy-start.2
  5.0 0.7 copy-start.3
  5.7 0.7 copy-start.4
  6.3 0.7 copy-start.5
  7.0 0.7 copy-start.6
  7.7 89.2 %copy-start = (s32[256,1]{1,0:T(8,128)}, s32[256,1]{1,0:T(8,128)S(1)}, u32[]{:S(2)}) copy-start(s32[256,1]{1,0:T(8,128)S(1)} %copy.17.ids_ref.ids_col_ref) | copy-start | bytes 3076

commit v3 on v2

--- a/solution.py
+++ b/solution.py
@@ -30,6 +30,24 @@
 
 def request_base(code):
     return jnp.where(code >= 2 * SPAN, 2 * SPAN, jnp.where(code >= SPAN, SPAN, 0))
+
+
+class View:
+    def __init__(self, ref, base, shape):
+        self.ref, self.base, self.shape = ref, base, shape
+
+    def __getitem__(self, index):
+        if isinstance(index, tuple):
+            index = index[0] * self.shape[1] + index[1]
+        return self.ref[self.base + index]
+
+
+def views(meta_ref, sizes):
+    slots, requests, groups = sizes
+    return (
+        View(meta_ref, 0, (slots,)), View(meta_ref, slots, (requests,)),
+        View(meta_ref, slots + requests, (groups, slots)),
+    )
 
 
 class Layout:
@@ -87,14 +105,13 @@
 
 
 def make_attention(
-    selected, owners_ref, counts_ref, table_ref, heads_ref, pages_ref, pcos_ref, psin_ref,
-    ids_col_ref, ids_row_ref, attended, keys, values, key_codes, row_codes, row_bases, queries, total,
+    selected, layout, table_ref, heads_ref, pages_ref, pcos_ref, psin_ref,
+    ids_col_ref, ids_row_ref, attended, keys, values, key_codes, row_codes, row_bases, queries, totals,
 ):
     rows = heads_ref.shape[1]
     groups, stretch = pages_ref.shape[:2]
     cached = groups * stretch
     group = lax.axis_index("grp")
-    layout = Layout(owners_ref, counts_ref, stretch)
     lane = lax.broadcasted_iota(jnp.int32, (1, stretch), 1)
     below = lax.broadcasted_iota(jnp.int32, (stretch, 1), 0)
     ids_col = ids_col_ref[...]
@@ -103,38 +120,40 @@
     def put_codes(i, codes):
         key_codes[i // per, :, pl.ds((i % per) * stretch, stretch)] = codes
 
-    for c in range(groups):
-        page = table_ref[group, c]
-        source = page // (table_ref.shape[1])
-        part = pl.ds(c * stretch, stretch)
-        turn = layout.offsets[c]
-        k = pages_ref[source, :, :HEAD].astype(jnp.float32)
-        k = turned(k, pcos_ref[pl.ds(turn, 1), :], psin_ref[pl.ds(turn, 1), :])
-        keys[part, :] = k.astype(jnp.bfloat16)
-        values[part, :HEAD] = pages_ref[source, :, HEAD:]
-        ids = lane + c * stretch
-        dead = jnp.max((ids_col == ids).astype(jnp.int32), axis=0, keepdims=True)
-        put_codes(c, jnp.where(dead > 0, FAR, ids + layout.slot_bases[c]))
-    keys[pl.ds(cached, rows), :] = heads_ref[2]
-    values[pl.ds(cached, rows), :HEAD] = heads_ref[3]
-    values[:, HEAD:] = jnp.ones((cached + rows, HEAD), jnp.bfloat16)
-    for i in range(rows // stretch):
-        by_lane = layout.of_queries(lane + (i * stretch - selected))
-        by_row = layout.of_queries(below + (i * stretch - selected))
-        if i == 0:
-            by_lane = jnp.where(lane < selected, layout.of_cached(ids_row_ref[...]), by_lane)
-            by_row = jnp.where(below < selected, layout.of_cached(ids_col), by_row)
-        put_codes(groups + i, by_lane)
-        row_codes[pl.ds(i * stretch, stretch), :] = by_row
-        row_bases[pl.ds(i * stretch, stretch), :] = request_base(by_row)
+    def lay_cached():
+        for c in range(groups):
+            page = table_ref[group, c]
+            source = page // (table_ref.shape[1])
+            part = pl.ds(c * stretch, stretch)
+            turn = layout.offsets[c]
+            k = pages_ref[source, :, :HEAD].astype(jnp.float32)
+            k = turned(k, pcos_ref[pl.ds(turn, 1), :], psin_ref[pl.ds(turn, 1), :])
+            keys[part, :] = k.astype(jnp.bfloat16)
+            values[part, :HEAD] = pages_ref[source, :, HEAD:]
+            ids = lane + c * stretch
+            dead = jnp.max((ids_col == ids).astype(jnp.int32), axis=0, keepdims=True)
+            put_codes(c, jnp.where(dead > 0, FAR, ids + layout.slot_bases[c]))
+
+    def lay_new():
+        keys[pl.ds(cached, rows), :] = heads_ref[2]
+        values[pl.ds(cached, rows), :HEAD] = heads_ref[3]
+        values[:, HEAD:] = jnp.ones((cached + rows, HEAD), jnp.bfloat16)
+        for i in range(rows // stretch):
+            by_lane = layout.of_queries(lane + (i * stretch - selected))
+            by_row = layout.of_queries(below + (i * stretch - selected))
+            if i == 0:
+                by_lane = jnp.where(lane < selected, layout.of_cached(ids_row_ref[...]), by_lane)
+                by_row = jnp.where(below < selected, layout.of_cached(ids_col), by_row)
+            put_codes(groups + i, by_lane)
+            row_codes[pl.ds(i * stretch, stretch), :] = by_row
+            row_bases[pl.ds(i * stretch, stretch), :] = request_base(by_row)
 
     ahead = cached // BLOCK
 
-    def row_block(rb):
+    def attend(rb, first, last):
         here = pl.ds(pl.multiple_of(rb * BLOCK, BLOCK), BLOCK)
         queries[:BLOCK, :] = heads_ref[0, here, :]
         queries[BLOCK:, :] = heads_ref[1, here, :]
-        total[...] = jnp.zeros_like(total)
         code = row_codes[here, :]
         base = row_bases[here, :]
 
@@ -150,22 +169,31 @@
             seen = (key_code <= code) & (key_code >= base)
             both = jnp.concatenate([seen, seen], axis=0)
             rounded = jnp.where(both, weights, 0.0).astype(jnp.bfloat16)
-            total[...] += jnp.dot(rounded, values[there, :], preferred_element_type=jnp.float32)
+            totals[rb] += jnp.dot(rounded, values[there, :], preferred_element_type=jnp.float32)
             return carry
 
-        lax.fori_loop(0, ahead + rb + 1, key_block, 0)
-        quotient = total[:, :HEAD] / total[:, HEAD:]
+        lax.fori_loop(first, last, key_block, 0)
+
+    def see_new(rb):
+        totals[rb] = jnp.zeros(totals.shape[1:], jnp.float32)
+        attend(rb, ahead, ahead + rb + 1)
+
+    def see_cached(rb):
+        attend(rb, 0, ahead)
+        here = pl.ds(pl.multiple_of(rb * BLOCK, BLOCK), BLOCK)
+        quotient = totals[rb, :, :HEAD] / totals[rb, :, HEAD:]
         attended[here, :HEAD] = quotient[:BLOCK].astype(jnp.bfloat16)
         attended[here, HEAD:] = quotient[BLOCK:].astype(jnp.bfloat16)
 
-    return row_block
+    return lay_new, lay_cached, see_new, see_cached
 
 
 def project_kernel(
-    selected, owners_ref, counts_ref, table_ref, heads_ref, pages_ref, pcos_ref, psin_ref,
+    selected, sizes, meta_ref, heads_ref, ck_ref, cv_ref, pcos_ref, psin_ref,
     ids_col_ref, ids_row_ref, w0_ref, hid_ref, gain_ref, out_ref,
-    attn_ref, keys, values, key_codes, row_codes, row_bases, queries, total, w1_ref, other, product, own, pair_out, pair_in, ring_out, ring_in, result,
-    other_send, other_recv, pair_send, pair_recv, ring_send, ring_recv, o_send, o_recv,
+    pages_ref, outgoing, attn_ref, keys, values, key_codes, row_codes, row_bases, queries, totals,
+    w1_ref, other, product, own, pair_out, pair_in, ring_out, ring_in, result,
+    other_send, other_recv, pair_send, pair_recv, ring_send, ring_recv, o_send, o_recv, p_send, p_recv,
 ):
     group, half, spot, core = place()
     rows = hid_ref.shape[0]
@@ -180,10 +208,17 @@
     ]
     near = device((1 - lows) * AROUND + depth, 1 - half, spot, core)
     beside = device((1 - lows) * AROUND + depth, half, spot, core)
+    offsets = [(0, 1), (0, -1), (1, 0), (0, 2), (1, 1), (1, -1), (1, 2)]
+
+    def group_at(low, deep):
+        return lax.rem(lows + low, 2) * AROUND + lax.rem(depth + deep + AROUND, AROUND)
+
     greet(
         [across, sibling, device(group, half, spot + 1, core), device(group, half, spot - 1, core)]
-        + zs + [near, beside]
+        + zs + [near, beside] + [device(group_at(*o), half, spot, core) for o in offsets[3:]]
     )
+    owners_ref, counts_ref, table_ref = views(meta_ref, sizes)
+    pages, stretch = ck_ref.shape[:2]
 
     def o_copy(i, src, step, n, to):
         size = w0_ref.shape[0] // (2 * AROUND)
@@ -196,10 +231,33 @@
 
     first, second = lows, 1 - lows
     o_copy(0, w0_ref, 0, second, near).start()
-    row_block = make_attention(
-        selected, owners_ref, counts_ref, table_ref, heads_ref, pages_ref, pcos_ref, psin_ref,
-        ids_col_ref, ids_row_ref, attn_ref, keys, values, key_codes, row_codes, row_bases, queries,
-        total,
+
+    def picked(target):
+        index = 0
+        for c in range(table_ref.shape[1]):
+            page = table_ref[target, c]
+            index = index + jnp.where(page // pages == group, page % pages, 0)
+        return index
+
+    def p_copy(j, source):
+        return pltpu.make_async_remote_copy(
+            src_ref=outgoing.at[j], dst_ref=pages_ref.at[source], send_sem=p_send.at[j],
+            recv_sem=p_recv.at[j], device_id=device(group_at(*offsets[j]), half, spot, core),
+            device_id_type=MESH,
+        )
+
+    for j, offset in enumerate(offsets):
+        index = picked(group_at(*offset))
+        outgoing[j, :, :HEAD] = ck_ref[index]
+        outgoing[j, :, HEAD:] = cv_ref[index]
+        p_copy(j, group).start()
+    index = picked(group)
+    pages_ref[group, :, :HEAD] = ck_ref[index]
+    pages_ref[group, :, HEAD:] = cv_ref[index]
+    lay_new, lay_cached, see_new, see_cached = make_attention(
+        selected, Layout(owners_ref, counts_ref, stretch), table_ref, heads_ref, pages_ref,
+        pcos_ref, psin_ref, ids_col_ref, ids_row_ref, attn_ref, keys, values, key_codes, row_codes,
+        row_bases, queries, totals,
     )
 
     def other_copy(j):
@@ -227,30 +285,34 @@
 
     per_half = attn_ref.shape[0] // BLOCK // 2
 
-    def attend(base_half, first_block):
+    def blocks_of(one_half, see):
         def step(i, carry):
-            row_block(base_half * per_half + i)
+            see(one_half * per_half + i)
             return carry
 
-        lax.fori_loop(first_block, first_block + 1, step, 0)
-
-    attend(1 - half, 0)
+        lax.fori_loop(0, per_half, step, 0)
+
+    lay_new()
+    blocks_of(half, see_new)
     o_copy(0, w1_ref, 0, first, near).wait_recv()
     o_copy(1, w1_ref, 0, first, beside).start()
     for d in range(2):
         o_copy(2 + d, w1_ref, 0, first, zs[d]).start()
-    attend(1 - half, 1)
-    for j in range(4):
-        other_copy(j).start()
+    blocks_of(1 - half, see_new)
     o_copy(1, w1_ref, 0, second, beside).wait_recv()
     for d in range(2):
         o_copy(4 + d, w1_ref, 0, second, zs[d]).start()
+    for j, (low, deep) in enumerate(offsets):
+        p_copy(j, group_at(low, -deep)).wait()
+    lay_cached()
     o_copy(2, w1_ref, -1, first, zs[0]).wait_recv()
     o_copy(6, w1_ref, -1, first, zs[0]).start()
-    attend(half, 0)
+    blocks_of(1 - half, see_cached)
+    for j in range(4):
+        other_copy(j).start()
     o_copy(5, w1_ref, 1, second, zs[1]).wait_recv()
     o_copy(7, w1_ref, 1, second, zs[1]).start()
-    attend(half, 1)
+    blocks_of(half, see_cached)
     o_copy(3, w1_ref, 1, first, zs[1]).wait_recv()
     o_copy(4, w1_ref, -1, second, zs[0]).wait_recv()
     o_copy(6, w1_ref, 2, first, zs[0]).wait_recv()
@@ -326,11 +388,13 @@
     ).astype(jnp.bfloat16)
 
 
-def project(heads, pages, owners, counts, table, selected, ids_col, ids_row, w_own, own_rows, post_gain):
+def project(
+    heads, cache_keys, cache_values, meta, sizes, selected, ids_col, ids_row, w_own, own_rows, post_gain
+):
     rows, features = own_rows.shape
     width = features // RINGS
     new_rows = heads.shape[1]
-    groups, stretch = pages.shape[:2]
+    groups, stretch = sizes[2], cache_keys.shape[1]
     total_keys = groups * stretch + new_rows
     angles = (np.arange(groups, dtype=np.float32) * stretch)[:, None] * frequencies()[None, :]
     cosine, sine = np.cos(angles), np.sin(angles)
@@ -338,11 +402,13 @@
     smem = pl.BlockSpec(memory_space=pltpu.SMEM)
     dma = pltpu.SemaphoreType.DMA
     return pl.pallas_call(
-        functools.partial(project_kernel, selected),
+        functools.partial(project_kernel, selected, sizes),
         out_shape=jax.ShapeDtypeStruct((rows, features), jnp.bfloat16),
-        in_specs=[smem] * 3 + [vmem] * 9,
+        in_specs=[smem] + [vmem] * 10,
         out_specs=vmem,
         scratch_shapes=[
+            pltpu.VMEM((groups, stretch, 2 * HEAD), jnp.bfloat16),
+            pltpu.VMEM((groups - 1, stretch, 2 * HEAD), jnp.bfloat16),
             pltpu.VMEM((new_rows, 2 * HEAD), jnp.bfloat16),
             pltpu.VMEM((total_keys, HEAD), jnp.bfloat16),
             pltpu.VMEM((total_keys, 2 * HEAD), jnp.bfloat16),
@@ -350,7 +416,7 @@
             pltpu.VMEM((new_rows, 1), jnp.int32),
             pltpu.VMEM((new_rows, 1), jnp.int32),
             pltpu.VMEM((2 * BLOCK, HEAD), jnp.bfloat16),
-            pltpu.VMEM((2 * BLOCK, 2 * HEAD), jnp.float32),
+            pltpu.VMEM((new_rows // BLOCK, 2 * BLOCK, 2 * HEAD), jnp.float32),
             pltpu.VMEM(w_own.shape, jnp.bfloat16),
             pltpu.VMEM((4, 2 * rows, 2 * HEAD), jnp.bfloat16),
             pltpu.VMEM((2 * rows, width), jnp.float32),
@@ -361,32 +427,31 @@
             pltpu.VMEM((3, RINGS, rows, width), jnp.bfloat16),
             pltpu.VMEM((rows, features), jnp.float32),
             dma((4,)), dma((4,)), dma((4, RINGS)), dma((4, RINGS)), dma((3, RINGS)), dma((3, RINGS)),
-            dma((8,)), dma((8,)),
+            dma((8,)), dma((8,)), dma((7,)), dma((7,)),
         ],
         compiler_params=pltpu.CompilerParams(
             collective_id=1, has_side_effects=True, vmem_limit_bytes=60 << 20
         ),
         name="project",
     )(
-        owners, counts, table, heads, pages,
+        meta, heads, cache_keys, cache_values,
         np.concatenate([cosine, cosine], axis=1), np.concatenate([-sine, sine], axis=1),
         ids_col, ids_row, w_own, own_rows, post_gain[None, :],
     )
 
 
 def project_in_kernel(
-    selected, owners_ref, counts_ref, table_ref, hid_ref, gain_ref, freq_ref, ids_ref,
-    wq_hbm, wk_hbm, wv_hbm, ck_hbm, cv_hbm,
-    heads_ref, pages_ref,
-    normed, weights, ship, wq_ref, wk_ref, wv_ref, ck_ref, cv_ref, outgoing, cos_ref, sin_ref,
-    l_sem, p_send, p_recv, x_send, x_recv, f_send, f_recv, s_send, s_recv, y_send, y_recv, w_send, w_recv, z_send, z_recv,
+    selected, sizes, stretch, meta_ref, hid_ref, gain_ref, freq_ref, ids_ref,
+    wq_hbm, wk_hbm, wv_hbm, heads_ref,
+    normed, weights, ship, wq_ref, wk_ref, wv_ref, cos_ref, sin_ref,
+    l_sem, x_send, x_recv, f_send, f_recv, s_send, s_recv, y_send, y_recv, w_send, w_recv, z_send, z_recv,
     g_send, g_recv, e_send, e_recv,
 ):
     group, half, spot, core = place()
     rows, features = hid_ref.shape
     depth = group % AROUND
     lows = group // AROUND
-    quarter = features // 4
+    quarter = features // 8
 
     def around(value):
         return lax.rem(value + 2 * AROUND, AROUND)
@@ -400,23 +465,16 @@
     across = device(group, 1 - half, spot, core)
     beside = device((1 - lows) * AROUND + depth, half, spot, core)
     sibling = device(group, half, spot, 1 - core)
-    offsets = [(0, 1), (0, -1), (1, 0), (0, 2), (1, 1), (1, -1), (1, 2)]
-
-    def group_at(low, deep):
-        return lax.rem(lows + low, 2) * AROUND + around(depth + deep)
-
     local = [
         pltpu.make_async_copy(src, dst, l_sem.at[i])
         for i, (src, dst) in enumerate(
-            [(ck_hbm, ck_ref), (cv_hbm, cv_ref), (wq_hbm, wq_ref), (wk_hbm, wk_ref), (wv_hbm, wv_ref)]
+            [(wq_hbm, wq_ref), (wk_hbm, wk_ref), (wv_hbm, wv_ref)]
         )
     ]
     for each in local:
         each.start()
-    greet(
-        xs + zs + [near, across, beside, sibling]
-        + [device(group_at(*o), half, spot, core) for o in offsets[3:]]
-    )
+    greet(xs + zs + [near, across, beside, sibling])
+    owners_ref, counts_ref, _ = views(meta_ref, sizes)
 
     def copy(src, dst, send, recv, to):
         return pltpu.make_async_remote_copy(
@@ -440,13 +498,13 @@
         piece = block(owner, base=base)
         return copy(piece, piece, s_send.at[i], s_recv.at[i], sibling)
 
-    mine_first, theirs_first = 2 * lows, 2 * (1 - lows)
+    mine_first, theirs_first = 4 * lows, 4 * (1 - lows)
 
     def slab(q, p):
         return weights.at[q, pl.ds(pl.multiple_of(p * quarter, quarter), quarter)]
 
     def y_start(j):
-        piece = (theirs_first if j < 2 else mine_first) + j % 2
+        piece = (theirs_first if j < 4 else mine_first) + j % 4
         part = pl.ds(pl.multiple_of(piece * quarter, quarter), quarter)
         sources = [
             wq_hbm.at[part, pl.ds(0, HEAD)], wq_hbm.at[part, pl.ds(HEAD, HEAD)],
@@ -465,43 +523,15 @@
         return copy(slab(q, p), slab(q, p), w_send.at[i], w_recv.at[i], beside)
 
     def nth_piece(n):
-        return (mine_first if n < 2 else theirs_first) + n % 2
+        return (mine_first if n < 4 else theirs_first) + n % 4
 
     def z_copy(d, n, q=depth):
         piece = slab(q, nth_piece(n))
         return copy(piece, piece, z_send.at[d, n], z_recv.at[d, n], zs[d])
 
-    def g_copy(d, q):
-        piece = slab(q, mine_first + d)
-        return copy(piece, piece, g_send.at[d], g_recv.at[d], zs[d])
-
-    pages, stretch = ck_ref.shape[:2]
-    groups = table_ref.shape[0]
-
-    def picked(target):
-        index = 0
-        for c in range(table_ref.shape[1]):
-            page = table_ref[target, c]
-            index = index + jnp.where(page // pages == group, page % pages, 0)
-        return index
-
-    def p_copy(j, source):
-        return copy(
-            outgoing.at[j], pages_ref.at[source], p_send.at[j], p_recv.at[j],
-            device(group_at(*offsets[j]), half, spot, core),
-        )
-
-    def send_pages():
-        for each in local[:2]:
-            each.wait()
-        for j, offset in enumerate(offsets):
-            index = picked(group_at(*offset))
-            outgoing[j, :, :HEAD] = ck_ref[index]
-            outgoing[j, :, HEAD:] = cv_ref[index]
-            p_copy(j, group).start()
-        index = picked(group)
-        pages_ref[group, :, :HEAD] = ck_ref[index]
-        pages_ref[group, :, HEAD:] = cv_ref[index]
+    def g_copy(d, j, q):
+        piece = slab(q, mine_first + 2 * d + j)
+        return copy(piece, piece, g_send.at[d, j], g_recv.at[d, j], zs[d])
 
     def make_tables():
         layout = Layout(owners_ref, counts_ref, stretch)
@@ -568,6 +598,13 @@
 
     left, right, far = owners[1], owners[2], owners[3]
     below, above, beyond = quarters[1], quarters[2], quarters[3]
+    def pass_on(n):
+        y_done(n).wait_recv()
+        z_copy(0, n).start()
+        z_copy(1, n).start()
+        if n + 2 < 8:
+            y_start(n + 2)
+
     y_start(0)
     y_start(1)
     wide = hid_ref[...].astype(jnp.float32)
@@ -576,54 +613,53 @@
     x_copy(0).start()
     x_copy(1).start()
     s_copy(0, spot).start()
-    send_pages()
+    pass_on(0)
+    pass_on(1)
     make_tables()
-    for each in local[2:]:
+    pass_on(2)
+    pass_on(3)
+    for each in local:
         each.wait()
-    for n in range(2):
-        y_done(n).wait_recv()
-        z_copy(0, n).start()
-        z_copy(1, n).start()
-        y_start(n + 2)
     s_copy(0, spot, twin).wait_recv()
     own_blocks(0, 1)
-    for n in range(2):
-        y_done(n + 2).wait_recv()
-        z_copy(0, n + 2).start()
-        z_copy(1, n + 2).start()
-    their_blocks(0, 1, 0, 1)
-    z_copy(0, 0, below).wait_recv()
-    g_copy(0, below).start()
-    z_copy(1, 1, above).wait_recv()
-    g_copy(1, above).start()
+    pass_on(4)
+    for j in range(2):
+        z_copy(0, j, below).wait_recv()
+        g_copy(0, j, below).start()
+    pass_on(5)
+    for j in range(2):
+        z_copy(1, 2 + j, above).wait_recv()
+        g_copy(1, j, above).start()
+    pass_on(6)
+    pass_on(7)
     x_copy(0, left).wait_recv()
     f_copy(0, left).start()
     s_copy(1, left).start()
     x_copy(1, right).wait_recv()
     f_copy(1, right).start()
     s_copy(2, right).start()
+    their_blocks(0, 1, 0, 1)
     s_copy(1, left, twin).wait_recv()
     s_copy(2, right, twin).wait_recv()
     their_blocks(0, 1, 1, 3)
-    for n in range(1, 4):
+    for d in range(2):
+        for j in range(2):
+            g_copy(d, j, beyond).wait_recv()
+            w_copy(2 * d + j, beyond, mine_first + 2 * d + j).start()
+    for n in range(2, 8):
         z_copy(0, n, below).wait_recv()
-    for n in (0, 2, 3):
+    for n in (0, 1, 4, 5, 6, 7):
         z_copy(1, n, above).wait_recv()
-    g_copy(0, beyond).wait_recv()
-    w_copy(0, beyond, mine_first).start()
-    g_copy(1, beyond).wait_recv()
-    w_copy(1, beyond, mine_first + 1).start()
-    their_blocks(1, 3, 0, 3)
-    own_blocks(1, 3)
-    w_copy(0, beyond, theirs_first).wait_recv()
-    w_copy(1, beyond, theirs_first + 1).wait_recv()
-    their_blocks(3, 4, 0, 3)
     f_copy(0, far).wait_recv()
     f_copy(1, far).wait_recv()
     s_copy(3, far).start()
+    their_blocks(1, 3, 0, 3)
     s_copy(3, far, twin).wait_recv()
-    their_blocks(0, 4, 3, 4)
-    own_blocks(3, 4)
+    their_blocks(0, 3, 3, 4)
+    for n in range(4):
+        w_copy(n, beyond, theirs_first + n).wait_recv()
+    their_blocks(3, 4, 0, 4)
+    own_blocks(1, 4)
     for i in range(4):
         for b in range(4):
             to = pl.ds(
@@ -635,59 +671,50 @@
     for d in range(2):
         x_copy(d).wait_send()
         f_copy(d, owners[1 + d]).wait_send()
-        for n in range(4):
+        for n in range(8):
             z_copy(d, n).wait_send()
-        g_copy(d, quarters[1 + d]).wait_send()
+        for j in range(2):
+            g_copy(d, j, quarters[1 + d]).wait_send()
     for i in range(4):
         s_copy(i, owners[i]).wait_send()
-    for n in range(2):
+    for n in range(4):
         w_copy(n, beyond, mine_first + n).wait_send()
-    for n in range(4):
+    for n in range(8):
         y_done(n).wait_send()
-    for j, (low, deep) in enumerate(offsets):
-        p_copy(j, group_at(low, -deep)).wait()
 
 
 def project_in(
-    own_rows, gain, w_query, w_key, w_value, cache_keys, cache_values,
-    owners, counts, table, selected, ids_col, new_rows,
+    own_rows, gain, w_query, w_key, w_value, meta, sizes, stretch, selected, ids_col, new_rows,
 ):
     rows, features = own_rows.shape
-    pages, stretch = cache_keys.shape[:2]
     vmem = pl.BlockSpec(memory_space=pltpu.VMEM)
     smem = pl.BlockSpec(memory_space=pltpu.SMEM)
     hbm = pl.BlockSpec(memory_space=pltpu.HBM)
     dma = pltpu.SemaphoreType.DMA
-    pairs = [(7,), (2,), (2,), (4,), (4,), (2,), (2, 4), (2,), (4, 4)]
+    pairs = [(2,), (2,), (4,), (8,), (4,), (2, 8), (2, 2), (4, 4)]
     bf16 = jnp.bfloat16
     return pl.pallas_call(
-        functools.partial(project_in_kernel, selected),
-        out_shape=(
-            jax.ShapeDtypeStruct((4, new_rows, HEAD), bf16),
-            jax.ShapeDtypeStruct((table.shape[0], stretch, 2 * HEAD), bf16),
-        ),
-        in_specs=[smem] * 3 + [vmem] * 4 + [hbm] * 5,
-        out_specs=(vmem, vmem),
+        functools.partial(project_in_kernel, selected, sizes, stretch),
+        out_shape=jax.ShapeDtypeStruct((4, new_rows, HEAD), bf16),
+        in_specs=[smem] + [vmem] * 4 + [hbm] * 3,
+        out_specs=vmem,
         scratch_shapes=[
             pltpu.VMEM((AROUND, 2 * rows, features), bf16),
             pltpu.VMEM((4, features, HEAD), bf16),
             pltpu.VMEM((4, 4, 2 * rows, HEAD), bf16),
             pltpu.VMEM(w_query.shape, bf16), pltpu.VMEM(w_key.shape, bf16),
             pltpu.VMEM(w_value.shape, bf16),
-            pltpu.VMEM(cache_keys.shape, bf16), pltpu.VMEM(cache_values.shape, bf16),
-            pltpu.VMEM((7, stretch, 2 * HEAD), bf16),
             pltpu.VMEM((new_rows // 2, HEAD), jnp.float32),
             pltpu.VMEM((new_rows // 2, HEAD), jnp.float32),
-            dma((5,)),
+            dma((3,)),
         ] + [dma(shape) for shape in pairs for _ in range(2)],
         compiler_params=pltpu.CompilerParams(
             collective_id=2, has_side_effects=True, vmem_limit_bytes=52 << 20
         ),
         name="project_in",
     )(
-        owners, counts, table, own_rows, gain[None, :],
-        np.concatenate([frequencies()] * 2)[None, :], ids_col,
-        w_query, w_key, w_value, cache_keys, cache_values,
+        meta, own_rows, gain[None, :], np.concatenate([frequencies()] * 2)[None, :], ids_col,
+        w_query, w_key, w_value,
     )
 
 
@@ -702,12 +729,13 @@
     selected = ids.shape[0]
     padded = jnp.pad(ids, (0, stretch - selected), constant_values=-1)
     ids_col, ids_row = padded[:, None], padded[None, :]
-    heads, pages = project_in(
-        own_rows, input_gain, w_query, w_key, w_value, cache_keys, cache_values,
-        owners, counts, page_table, selected, ids_col, new_rows,
+    sizes = (owners.shape[0], counts.shape[0], page_table.shape[0])
+    meta = jnp.concatenate([owners, counts, page_table.reshape(-1)])
+    heads = project_in(
+        own_rows, input_gain, w_query, w_key, w_value, meta, sizes, stretch, selected, ids_col, new_rows
     )
     output = project(
-        heads, pages, owners, counts, page_table, selected, ids_col, ids_row, w_out, own_rows,
+        heads, cache_keys, cache_values, meta, sizes, selected, ids_col, ids_row, w_out, own_rows,
         post_gain,
     )
     return output[None]

time: 179 us -> 175 us (0.978)
  Pallas kernels: 169 us -> 165 us
  local copies, waits for them, and re-layouts: 9.99 us -> 7.96 us
    pallas_call x2, Pallas kernels: 169 us -> 165 us  [the longest x1 86 us: project(): pl.pallas_call(functools.partial(project_kernel, selected, sizes), out_sh...]
    unnamed x17 -> x11, local copies, waits for them, and re-layouts: 7.1 us -> 4.3 us
where the time goes in v3:
time: 175 us; the launch traced here: 174 us
  Pallas kernels  165 us (94%)
  local copies, waits for them, and re-layouts  7.96 us (5%)
    pallas_call x1, Pallas kernels, project(): pl.pallas_call(functools.partial(project_kernel, selected, sizes), out_sh...  86 us
    pallas_call x1, Pallas kernels, project_in(): pl.pallas_call(functools.partial(project_in_kernel, selected, sizes, stre...  79.4 us
    unnamed x11, local copies, waits for them, and re-layouts  4.3 us

profile of v3, /device:TPU:1, one launch (start us, length us, event | category | flops | bytes accessed | tf_op | source)
XLA Modules:
  0.0 174.2 jit_solution(16968227856397342305)
XLA Ops:
  0.0 0.8 reshape.3
  0.8 0.7 pad_add_fusion.meta_ref
  1.5 0.0 copy-start.2
  1.5 0.7 pad.4
  2.2 0.0 copy-start.4
  2.2 0.7 broadcast_in_dim.15.gain_ref
  2.9 1.3 broadcast_in_dim.18.gain_ref
  4.3 0.1 copy.17.ids_ref.ids_col_ref
  4.4 0.0 copy-start
  4.4 1.3 copy-done
  5.7 0.0 copy-start.3
  5.7 0.7 copy-done.3
  6.4 0.0 copy-start.1
  6.4 79.4 %project_in.1.heads_ref = bf16[4,2048,128]{2,1,0:T(8,128)(2,1)} custom-call(s32[75]{0:T(128)S(1)} %pad_add_fusion.meta_ref, bf16[128,4608]{1,0:T(8,128)(2,1)S(1)} %bitcast.8, f32[1,4608]{1,0:T(1,128)S(1)} %broadcast_in_dim.15.gain_ref, f32[1,128]{1,0:T(1,128)S(1)} %copy-done.3, s32[256,1]{1,0:T(8,128)S(1)} %copy.17.ids_ref.ids_col_ref, ...), custom_call_target="tpu_custom_call" | custom-call | tf_op jit(solution)/shard_map/project_in/pallas_call | solution.py:696
  85.8 0.0 copy-done.2
  85.8 0.0 copy-done.4
  85.8 0.0 copy-done.1
  85.8 86.0 %project.1 = bf16[128,4608]{1,0:T(8,128)(2,1)} custom-call(s32[75]{0:T(128)} %copy-done.2, bf16[4,2048,128]{2,1,0:T(8,128)(2,1)} %project_in.1.heads_ref, bf16[8,256,128]{2,1,0:T(8,128)(2,1)} %ck_ref.1, bf16[8,256,128]{2,1,0:T(8,128)(2,1)} %cv_ref.1, f32[8,128]{1,0:T(8,128)} %constant.9.clone.pcos_ref, f32[8,128]{1,0:T(8,128)} %constant.10.clone.psin_ref, ...), custom_call_target="tpu_custom_call" | custom-call | tf_op jit(solution)/shard_map/project/pallas_call | solution.py:404
  171.8 2.4 %copy.20 = bf16[1,128,4608]{2,1,0:T(8,128)(2,1)} copy(bf16[1,128,4608]{2,1,0:T(8,128)(2,1)} %bitcast.9) | data formatting | bytes 2359296
Async XLA Ops:
  1.5 84.3 %copy-start.2 = (s32[75]{0:T(128)}, s32[75]{0:T(128)S(1)}, u32[]{:S(2)}) copy-start(s32[75]{0:T(128)S(1)} %pad_add_fusion.meta_ref) | copy-start | bytes 904
  2.2 83.6 %copy-start.4 = (s32[256]{0:T(256)}, s32[256]{0:T(256)S(1)}, u32[]{:S(2)}) copy-start(s32[256]{0:T(256)S(1)} %pad.4) | copy-start | bytes 3076
  4.4 1.3 copy-start
  5.7 0.7 copy-start.3
  6.4 79.4 %copy-start.1 = (s32[256,1]{1,0:T(8,128)}, s32[256,1]{1,0:T(8,128)S(1)}, u32[]{:S(2)}) copy-start(s32[256,1]{1,0:T(8,128)S(1)} %copy.17.ids_ref.ids_col_ref) | copy-start | bytes 3076

commit v4 on v3

--- a/solution.py
+++ b/solution.py
@@ -106,7 +106,7 @@
 
 def make_attention(
     selected, layout, table_ref, heads_ref, pages_ref, pcos_ref, psin_ref,
-    ids_col_ref, ids_row_ref, attended, keys, values, key_codes, row_codes, row_bases, queries, totals,
+    ids_col_ref, ids_row_ref, attended, keys, values, cached_codes, key_codes, row_codes, row_bases, queries, totals,
 ):
     rows = heads_ref.shape[1]
     groups, stretch = pages_ref.shape[:2]
@@ -115,10 +115,11 @@
     lane = lax.broadcasted_iota(jnp.int32, (1, stretch), 1)
     below = lax.broadcasted_iota(jnp.int32, (stretch, 1), 0)
     ids_col = ids_col_ref[...]
-    per = BLOCK // stretch
-
-    def put_codes(i, codes):
-        key_codes[i // per, :, pl.ds((i % per) * stretch, stretch)] = codes
+    wide = cached_codes.shape[2]
+
+    def put_codes(codes_ref, i, codes):
+        per = codes_ref.shape[2] // stretch
+        codes_ref[i // per, :, pl.ds((i % per) * stretch, stretch)] = codes
 
     def lay_cached():
         for c in range(groups):
@@ -132,7 +133,7 @@
             values[part, :HEAD] = pages_ref[source, :, HEAD:]
             ids = lane + c * stretch
             dead = jnp.max((ids_col == ids).astype(jnp.int32), axis=0, keepdims=True)
-            put_codes(c, jnp.where(dead > 0, FAR, ids + layout.slot_bases[c]))
+            put_codes(cached_codes, c, jnp.where(dead > 0, FAR, ids + layout.slot_bases[c]))
 
     def lay_new():
         keys[pl.ds(cached, rows), :] = heads_ref[2]
@@ -144,56 +145,66 @@
             if i == 0:
                 by_lane = jnp.where(lane < selected, layout.of_cached(ids_row_ref[...]), by_lane)
                 by_row = jnp.where(below < selected, layout.of_cached(ids_col), by_row)
-            put_codes(groups + i, by_lane)
+            put_codes(key_codes, i, by_lane)
             row_codes[pl.ds(i * stretch, stretch), :] = by_row
             row_bases[pl.ds(i * stretch, stretch), :] = request_base(by_row)
 
-    ahead = cached // BLOCK
-
-    def attend(rb, first, last):
+    def weigh(asked, there, key_code, code, base):
+        scores = lax.dot_general(
+            asked, keys[there, :], (((1,), (1,)), ((), ())), preferred_element_type=jnp.float32
+        )
+        capped = jnp.tanh(scores * (QUERY_SCALE / CAP_VALUE))
+        weights = jnp.exp2(capped * (CAP_VALUE * math.log2(math.e)))
+        seen = (key_code <= code) & (key_code >= base)
+        both = jnp.concatenate([seen, seen], axis=0)
+        rounded = jnp.where(both, weights, 0.0).astype(jnp.bfloat16)
+        return jnp.dot(rounded, values[there, :], preferred_element_type=jnp.float32)
+
+    def see_new(rb):
         here = pl.ds(pl.multiple_of(rb * BLOCK, BLOCK), BLOCK)
         queries[:BLOCK, :] = heads_ref[0, here, :]
         queries[BLOCK:, :] = heads_ref[1, here, :]
-        code = row_codes[here, :]
-        base = row_bases[here, :]
+        code, base = row_codes[here, :], row_bases[here, :]
+        totals[rb] = jnp.zeros(totals.shape[1:], jnp.float32)
 
         def key_block(kb, carry):
-            there = pl.ds(pl.multiple_of(kb * BLOCK, BLOCK), BLOCK)
-            scores = lax.dot_general(
-                queries[...], keys[there, :], (((1,), (1,)), ((), ())),
-                preferred_element_type=jnp.float32,
-            )
-            capped = jnp.tanh(scores * (QUERY_SCALE / CAP_VALUE))
-            weights = jnp.exp2(capped * (CAP_VALUE * math.log2(math.e)))
-            key_code = key_codes[kb]
-            seen = (key_code <= code) & (key_code >= base)
-            both = jnp.concatenate([seen, seen], axis=0)
-            rounded = jnp.where(both, weights, 0.0).astype(jnp.bfloat16)
-            totals[rb] += jnp.dot(rounded, values[there, :], preferred_element_type=jnp.float32)
+            there = pl.ds(pl.multiple_of(cached + kb * BLOCK, BLOCK), BLOCK)
+            totals[rb] += weigh(queries[...], there, key_codes[kb], code, base)
             return carry
 
-        lax.fori_loop(first, last, key_block, 0)
-
-    def see_new(rb):
-        totals[rb] = jnp.zeros(totals.shape[1:], jnp.float32)
-        attend(rb, ahead, ahead + rb + 1)
-
-    def see_cached(rb):
-        attend(rb, 0, ahead)
-        here = pl.ds(pl.multiple_of(rb * BLOCK, BLOCK), BLOCK)
-        quotient = totals[rb, :, :HEAD] / totals[rb, :, HEAD:]
-        attended[here, :HEAD] = quotient[:BLOCK].astype(jnp.bfloat16)
-        attended[here, HEAD:] = quotient[BLOCK:].astype(jnp.bfloat16)
+        lax.fori_loop(0, rb + 1, key_block, 0)
+
+    def see_cached(qb):
+        few = BLOCK // 2
+        here = pl.ds(pl.multiple_of(qb * few, few), few)
+        queries[:few, :] = heads_ref[0, here, :]
+        queries[few:BLOCK, :] = heads_ref[1, here, :]
+        code, base = row_codes[here, :], row_bases[here, :]
+        rb = qb // 2
+        low = pl.ds(pl.multiple_of(lax.rem(qb, 2) * few, few), few)
+        high = pl.ds(pl.multiple_of(BLOCK + lax.rem(qb, 2) * few, few), few)
+
+        def key_block(kb, carry):
+            there = pl.ds(pl.multiple_of(kb * wide, wide), wide)
+            more = weigh(queries[:BLOCK, :], there, cached_codes[kb], code, base)
+            totals[rb, low, :] += more[:few]
+            totals[rb, high, :] += more[few:]
+            return carry
+
+        lax.fori_loop(0, cached // wide, key_block, 0)
+        for head, part in enumerate((low, high)):
+            quotient = totals[rb, part, :HEAD] / totals[rb, part, HEAD:]
+            attended[here, head * HEAD : (head + 1) * HEAD] = quotient.astype(jnp.bfloat16)
 
     return lay_new, lay_cached, see_new, see_cached
 
 
 def project_kernel(
     selected, sizes, meta_ref, heads_ref, ck_ref, cv_ref, pcos_ref, psin_ref,
-    ids_col_ref, ids_row_ref, w0_ref, hid_ref, gain_ref, out_ref,
-    pages_ref, outgoing, attn_ref, keys, values, key_codes, row_codes, row_bases, queries, totals,
-    w1_ref, other, product, own, pair_out, pair_in, ring_out, ring_in, result,
-    other_send, other_recv, pair_send, pair_recv, ring_send, ring_recv, o_send, o_recv, p_send, p_recv,
+    ids_col_ref, ids_row_ref, w0_ref, w1_ref, hid_ref, gain_ref, out_ref,
+    pages_ref, outgoing, attn_ref, keys, values, cached_codes, key_codes, row_codes, row_bases,
+    queries, totals, other, product, own, pair_out, pair_in, ring_out, ring_in, result,
+    other_send, other_recv, pair_send, pair_recv, ring_send, ring_recv, p_send, p_recv,
 ):
     group, half, spot, core = place()
     rows = hid_ref.shape[0]
@@ -206,7 +217,6 @@
         device(lows * AROUND + lax.rem(depth + 1, AROUND), half, spot, core),
         device(lows * AROUND + lax.rem(depth + AROUND - 1, AROUND), half, spot, core),
     ]
-    near = device((1 - lows) * AROUND + depth, 1 - half, spot, core)
     beside = device((1 - lows) * AROUND + depth, half, spot, core)
     offsets = [(0, 1), (0, -1), (1, 0), (0, 2), (1, 1), (1, -1), (1, 2)]
 
@@ -215,22 +225,10 @@
 
     greet(
         [across, sibling, device(group, half, spot + 1, core), device(group, half, spot - 1, core)]
-        + zs + [near, beside] + [device(group_at(*o), half, spot, core) for o in offsets[3:]]
+        + zs + [beside] + [device(group_at(*o), half, spot, core) for o in offsets[3:]]
     )
     owners_ref, counts_ref, table_ref = views(meta_ref, sizes)
     pages, stretch = ck_ref.shape[:2]
-
-    def o_copy(i, src, step, n, to):
-        size = w0_ref.shape[0] // (2 * AROUND)
-        piece = lax.rem(depth + step + AROUND, AROUND) * 2 + n
-        part = pl.ds(pl.multiple_of(piece * size, size), size)
-        return pltpu.make_async_remote_copy(
-            src_ref=src.at[part], dst_ref=w1_ref.at[part], send_sem=o_send.at[i],
-            recv_sem=o_recv.at[i], device_id=to, device_id_type=MESH,
-        )
-
-    first, second = lows, 1 - lows
-    o_copy(0, w0_ref, 0, second, near).start()
 
     def picked(target):
         index = 0
@@ -256,12 +254,12 @@
     pages_ref[group, :, HEAD:] = cv_ref[index]
     lay_new, lay_cached, see_new, see_cached = make_attention(
         selected, Layout(owners_ref, counts_ref, stretch), table_ref, heads_ref, pages_ref,
-        pcos_ref, psin_ref, ids_col_ref, ids_row_ref, attn_ref, keys, values, key_codes, row_codes,
-        row_bases, queries, totals,
+        pcos_ref, psin_ref, ids_col_ref, ids_row_ref, attn_ref, keys, values, cached_codes, key_codes,
+        row_codes, row_bases, queries, totals,
     )
 
     def other_copy(j):
-        owner = lax.rem(spot + (3, 1, 2, 0)[j], AROUND)
+        owner = lax.rem(spot + 3 - 2 * j + 3 * (j // 2) + AROUND, AROUND)
         start = pl.multiple_of(((1 - half) * AROUND + owner) * chunk, chunk)
         return pltpu.make_async_remote_copy(
             src_ref=attn_ref.at[pl.ds(start, chunk)], dst_ref=other.at[j],
@@ -294,29 +292,27 @@
 
     lay_new()
     blocks_of(half, see_new)
-    o_copy(0, w1_ref, 0, first, near).wait_recv()
-    o_copy(1, w1_ref, 0, first, beside).start()
-    for d in range(2):
-        o_copy(2 + d, w1_ref, 0, first, zs[d]).start()
     blocks_of(1 - half, see_new)
-    o_copy(1, w1_ref, 0, second, beside).wait_recv()
-    for d in range(2):
-        o_copy(4 + d, w1_ref, 0, second, zs[d]).start()
     for j, (low, deep) in enumerate(offsets):
         p_copy(j, group_at(low, -deep)).wait()
     lay_cached()
-    o_copy(2, w1_ref, -1, first, zs[0]).wait_recv()
-    o_copy(6, w1_ref, -1, first, zs[0]).start()
-    blocks_of(1 - half, see_cached)
-    for j in range(4):
-        other_copy(j).start()
-    o_copy(5, w1_ref, 1, second, zs[1]).wait_recv()
-    o_copy(7, w1_ref, 1, second, zs[1]).start()
-    blocks_of(half, see_cached)
-    o_copy(3, w1_ref, 1, first, zs[1]).wait_recv()
-    o_copy(4, w1_ref, -1, second, zs[0]).wait_recv()
-    o_copy(6, w1_ref, 2, first, zs[0]).wait_recv()
-    o_copy(7, w1_ref, 2, second, zs[1]).wait_recv()
+
+    def finish_rows(first, last):
+        count = last - first
+
+        def step(n, carry):
+            theirs = n < count
+            j = first + lax.rem(n, count)
+            owner = lax.rem(spot + 3 - 2 * j + 3 * (j // 2) + AROUND, AROUND)
+            see_cached(jnp.where(theirs, 1 - half, half) * AROUND + owner)
+
+            @pl.when(theirs)
+            def _():
+                other_copy(j).start()
+
+            return carry
+
+        lax.fori_loop(0, 2 * count, step, 0)
 
     def partial(s, r):
         owner = lax.rem(spot + (2 * (r // 2) - 1) * (1 + s) + 2 * AROUND, AROUND)
@@ -355,23 +351,24 @@
         for r in (0, 2, 1, 3):
             step(r, 0)
 
+    finish_rows(0, 2)
     other_copy(0).wait_recv()
     partials(0, 0, 2)
     other_copy(1).wait_recv()
     partials(0, 2, 4)
     forward(0)
+    finish_rows(2, 3)
     other_copy(2).wait_recv()
     partials(1, 0, 4)
+    forward(1)
+    finish_rows(3, 4)
     partials(2, 0, 4)
+    forward(2)
     other_copy(3).wait_recv()
     partials(3, 0, 4)
-    forward(1)
-    forward(2)
     forward(3)
     for j in range(4):
         other_copy(j).wait_send()
-    for i in range(8):
-        o_copy(i, w1_ref, 0, first, near).wait_send()
 
     def drain(r, carry):
         for s in range(4):
@@ -389,7 +386,8 @@
 
 
 def project(
-    heads, cache_keys, cache_values, meta, sizes, selected, ids_col, ids_row, w_own, own_rows, post_gain
+    heads, cache_keys, cache_values, meta, sizes, selected, ids_col, ids_row, w_own, w_across, own_rows,
+    post_gain,
 ):
     rows, features = own_rows.shape
     width = features // RINGS
@@ -404,7 +402,7 @@
     return pl.pallas_call(
         functools.partial(project_kernel, selected, sizes),
         out_shape=jax.ShapeDtypeStruct((rows, features), jnp.bfloat16),
-        in_specs=[smem] + [vmem] * 10,
+        in_specs=[smem] + [vmem] * 11,
         out_specs=vmem,
         scratch_shapes=[
             pltpu.VMEM((groups, stretch, 2 * HEAD), jnp.bfloat16),
@@ -412,12 +410,12 @@
             pltpu.VMEM((new_rows, 2 * HEAD), jnp.bfloat16),
             pltpu.VMEM((total_keys, HEAD), jnp.bfloat16),
             pltpu.VMEM((total_keys, 2 * HEAD), jnp.bfloat16),
-            pltpu.VMEM((total_keys // BLOCK, 1, BLOCK), jnp.int32),
+            pltpu.VMEM((groups * stretch // (2 * BLOCK), 1, 2 * BLOCK), jnp.int32),
+            pltpu.VMEM((new_rows // BLOCK, 1, BLOCK), jnp.int32),
             pltpu.VMEM((new_rows, 1), jnp.int32),
             pltpu.VMEM((new_rows, 1), jnp.int32),
             pltpu.VMEM((2 * BLOCK, HEAD), jnp.bfloat16),
             pltpu.VMEM((new_rows // BLOCK, 2 * BLOCK, 2 * HEAD), jnp.float32),
-            pltpu.VMEM(w_own.shape, jnp.bfloat16),
             pltpu.VMEM((4, 2 * rows, 2 * HEAD), jnp.bfloat16),
             pltpu.VMEM((2 * rows, width), jnp.float32),
             pltpu.VMEM((4, RINGS, rows, width), jnp.float32),
@@ -427,7 +425,7 @@
             pltpu.VMEM((3, RINGS, rows, width), jnp.bfloat16),
             pltpu.VMEM((rows, features), jnp.float32),
             dma((4,)), dma((4,)), dma((4, RINGS)), dma((4, RINGS)), dma((3, RINGS)), dma((3, RINGS)),
-            dma((8,)), dma((8,)), dma((7,)), dma((7,)),
+            dma((7,)), dma((7,)),
         ],
         compiler_params=pltpu.CompilerParams(
             collective_id=1, has_side_effects=True, vmem_limit_bytes=60 << 20
@@ -436,16 +434,16 @@
     )(
         meta, heads, cache_keys, cache_values,
         np.concatenate([cosine, cosine], axis=1), np.concatenate([-sine, sine], axis=1),
-        ids_col, ids_row, w_own, own_rows, post_gain[None, :],
+        ids_col, ids_row, w_own, w_across, own_rows, post_gain[None, :],
     )
 
 
 def project_in_kernel(
     selected, sizes, stretch, meta_ref, hid_ref, gain_ref, freq_ref, ids_ref,
-    wq_hbm, wk_hbm, wv_hbm, heads_ref,
+    wq_hbm, wk_hbm, wv_hbm, wo_ref, heads_ref, wo_across_ref,
     normed, weights, ship, wq_ref, wk_ref, wv_ref, cos_ref, sin_ref,
     l_sem, x_send, x_recv, f_send, f_recv, s_send, s_recv, y_send, y_recv, w_send, w_recv, z_send, z_recv,
-    g_send, g_recv, e_send, e_recv,
+    g_send, g_recv, o_send, o_recv, e_send, e_recv,
 ):
     group, half, spot, core = place()
     rows, features = hid_ref.shape
@@ -532,6 +530,12 @@
     def g_copy(d, j, q):
         piece = slab(q, mine_first + 2 * d + j)
         return copy(piece, piece, g_send.at[d, j], g_recv.at[d, j], zs[d])
+
+    def o_copy(i, src, q, part, to):
+        size = wo_ref.shape[0] // (4 if part is None else 8)
+        start = q * (wo_ref.shape[0] // 4) + (part or 0) * size
+        piece = pl.ds(pl.multiple_of(start, size), size)
+        return copy(src.at[piece], wo_across_ref.at[piece], o_send.at[i], o_recv.at[i], to)
 
     def make_tables():
         layout = Layout(owners_ref, counts_ref, stretch)
@@ -632,6 +636,7 @@
         g_copy(1, j, above).start()
     pass_on(6)
     pass_on(7)
+    o_copy(0, wo_ref, depth, None, near).start()
     x_copy(0, left).wait_recv()
     f_copy(0, left).start()
     s_copy(1, left).start()
@@ -646,6 +651,9 @@
         for j in range(2):
             g_copy(d, j, beyond).wait_recv()
             w_copy(2 * d + j, beyond, mine_first + 2 * d + j).start()
+    o_copy(0, wo_ref, depth, None, near).wait_recv()
+    o_copy(1, wo_across_ref, depth, None, zs[0]).start()
+    o_copy(2, wo_across_ref, depth, None, zs[1]).start()
     for n in range(2, 8):
         z_copy(0, n, below).wait_recv()
     for n in (0, 1, 4, 5, 6, 7):
@@ -659,7 +667,14 @@
     for n in range(4):
         w_copy(n, beyond, theirs_first + n).wait_recv()
     their_blocks(3, 4, 0, 4)
-    own_blocks(1, 4)
+    own_blocks(1, 2)
+    o_copy(1, wo_across_ref, below, None, zs[0]).wait_recv()
+    o_copy(3, wo_across_ref, below, 0, zs[0]).start()
+    o_copy(2, wo_across_ref, above, None, zs[1]).wait_recv()
+    o_copy(4, wo_across_ref, above, 1, zs[1]).start()
+    own_blocks(2, 4)
+    o_copy(3, wo_across_ref, beyond, 0, zs[0]).wait_recv()
+    o_copy(4, wo_across_ref, beyond, 1, zs[1]).wait_recv()
     for i in range(4):
         for b in range(4):
             to = pl.ds(
@@ -681,23 +696,30 @@
         w_copy(n, beyond, mine_first + n).wait_send()
     for n in range(8):
         y_done(n).wait_send()
+    o_copy(0, wo_ref, depth, None, near).wait_send()
+    o_copy(1, wo_across_ref, depth, None, zs[0]).wait_send()
+    o_copy(2, wo_across_ref, depth, None, zs[1]).wait_send()
+    o_copy(3, wo_across_ref, below, 0, zs[0]).wait_send()
+    o_copy(4, wo_across_ref, above, 1, zs[1]).wait_send()
 
 
 def project_in(
-    own_rows, gain, w_query, w_key, w_value, meta, sizes, stretch, selected, ids_col, new_rows,
+    own_rows, gain, w_query, w_key, w_value, w_out, meta, sizes, stretch, selected, ids_col, new_rows,
 ):
     rows, features = own_rows.shape
     vmem = pl.BlockSpec(memory_space=pltpu.VMEM)
     smem = pl.BlockSpec(memory_space=pltpu.SMEM)
     hbm = pl.BlockSpec(memory_space=pltpu.HBM)
     dma = pltpu.SemaphoreType.DMA
-    pairs = [(2,), (2,), (4,), (8,), (4,), (2, 8), (2, 2), (4, 4)]
+    pairs = [(2,), (2,), (4,), (8,), (4,), (2, 8), (2, 2), (5,), (4, 4)]
     bf16 = jnp.bfloat16
     return pl.pallas_call(
         functools.partial(project_in_kernel, selected, sizes, stretch),
-        out_shape=jax.ShapeDtypeStruct((4, new_rows, HEAD), bf16),
-        in_specs=[smem] + [vmem] * 4 + [hbm] * 3,
-        out_specs=vmem,
+        out_shape=(
+            jax.ShapeDtypeStruct((4, new_rows, HEAD), bf16), jax.ShapeDtypeStruct(w_out.shape, bf16)
+        ),
+        in_specs=[smem] + [vmem] * 4 + [hbm] * 4,
+        out_specs=(vmem, hbm),
         scratch_shapes=[
             pltpu.VMEM((AROUND, 2 * rows, features), bf16),
             pltpu.VMEM((4, features, HEAD), bf16),
@@ -714,7 +736,7 @@
         name="project_in",
     )(
         meta, own_rows, gain[None, :], np.concatenate([frequencies()] * 2)[None, :], ids_col,
-        w_query, w_key, w_value,
+        w_query, w_key, w_value, w_out,
     )
 
 
@@ -731,11 +753,12 @@
     ids_col, ids_row = padded[:, None], padded[None, :]
     sizes = (owners.shape[0], counts.shape[0], page_table.shape[0])
     meta = jnp.concatenate([owners, counts, page_table.reshape(-1)])
-    heads = project_in(
-        own_rows, input_gain, w_query, w_key, w_value, meta, sizes, stretch, selected, ids_col, new_rows
+    heads, w_across = project_in(
+        own_rows, input_gain, w_query, w_key, w_value, w_out, meta, sizes, stretch, selected, ids_col,
+        new_rows,
     )
     output = project(
-        heads, cache_keys, cache_values, meta, sizes, selected, ids_col, ids_row, w_out, own_rows,
+        heads, cache_keys, cache_values, meta, sizes, selected, ids_col, ids_row, w_out, w_across, own_rows,
         post_gain,
     )
     return output[None]

time: 175 us -> 163 us (0.931)
  Pallas kernels: 165 us -> 154 us
    pallas_call x1, Pallas kernels: 86 us -> 74.4 us  [project(): pl.pallas_call(functools.partial(project_kernel, selected, sizes), out_sh...]
where the time goes in v4:
time: 163 us
  Pallas kernels  154 us (94%)
  local copies, waits for them, and re-layouts  7.96 us (5%)
    pallas_call x1, Pallas kernels, project_in(): pl.pallas_call(functools.partial(project_in_kernel, selected, sizes, stre...  79.5 us
    pallas_call x1, Pallas kernels, project(): pl.pallas_call(functools.partial(project_kernel, selected, sizes), out_sh...  74.4 us
    unnamed x11, local copies, waits for them, and re-layouts  4.3 us

profile of v4, /device:TPU:1, one launch (start us, length us, event | category | flops | bytes accessed | tf_op | source)
XLA Modules:
  0.0 162.6 jit_solution(4072205215739341428)
XLA Ops:
  0.0 0.8 reshape.3
  0.8 0.7 pad_add_fusion.meta_ref
  1.5 0.0 copy-start.2
  1.5 0.7 pad.4
  2.2 0.0 copy-start.4
  2.2 0.7 broadcast_in_dim.15.gain_ref
  2.9 1.3 broadcast_in_dim.18.gain_ref
  4.3 0.1 copy.17.ids_ref.ids_col_ref
  4.4 0.0 copy-start
  4.4 1.3 copy-done
  5.7 0.0 copy-start.3
  5.7 0.7 copy-done.3
  6.4 0.0 copy-start.1
  6.4 79.5 %project_in.1 = (bf16[4,2048,128]{2,1,0:T(8,128)(2,1)}, bf16[256,4608]{1,0:T(8,128)(2,1)}) custom-call(s32[75]{0:T(128)S(1)} %pad_add_fusion.meta_ref, bf16[128,4608]{1,0:T(8,128)(2,1)S(1)} %bitcast.8, f32[1,4608]{1,0:T(1,128)S(1)} %broadcast_in_dim.15.gain_ref, f32[1,128]{1,0:T(1,128)S(1)} %copy-done.3, s32[256,1]{1,0:T(8,128)S(1)} %copy.17.ids_ref.ids_col_ref, ...), custom_call_target="tpu_custom_call" | custom-call | tf_op jit(solution)/shard_map/project_in/pallas_call | solution.py:716
  85.8 0.0 copy-done.2
  85.8 0.0 copy-done.4
  85.9 0.0 copy-done.1
  85.9 74.4 %project.1 = bf16[128,4608]{1,0:T(8,128)(2,1)} custom-call(s32[75]{0:T(128)} %copy-done.2, bf16[4,2048,128]{2,1,0:T(8,128)(2,1)} %get-tuple-element.7.heads_ref, bf16[8,256,128]{2,1,0:T(8,128)(2,1)} %ck_ref.1, bf16[8,256,128]{2,1,0:T(8,128)(2,1)} %cv_ref.1, f32[8,128]{1,0:T(8,128)} %constant.9.clone.pcos_ref, f32[8,128]{1,0:T(8,128)} %constant.10.clone.psin_ref, ...), custom_call_target="tpu_custom_call" | custom-call | tf_op jit(solution)/shard_map/project/pallas_call | solution.py:402
  160.2 2.4 %copy.20 = bf16[1,128,4608]{2,1,0:T(8,128)(2,1)} copy(bf16[1,128,4608]{2,1,0:T(8,128)(2,1)} %bitcast.9) | data formatting | bytes 2359296
Async XLA Ops:
  1.5 84.3 %copy-start.2 = (s32[75]{0:T(128)}, s32[75]{0:T(128)S(1)}, u32[]{:S(2)}) copy-start(s32[75]{0:T(128)S(1)} %pad_add_fusion.meta_ref) | copy-start | bytes 904
  2.2 83.6 %copy-start.4 = (s32[256]{0:T(256)}, s32[256]{0:T(256)S(1)}, u32[]{:S(2)}) copy-start(s32[256]{0:T(256)S(1)} %pad.4) | copy-start | bytes 3076
  4.4 1.3 copy-start
  5.7 0.7 copy-start.3
  6.4 79.5 %copy-start.1 = (s32[256,1]{1,0:T(8,128)}, s32[256,1]{1,0:T(8,128)S(1)}, u32[]{:S(2)}) copy-start(s32[256,1]{1,0:T(8,128)S(1)} %copy.17.ids_ref.ids_col_ref) | copy-start | bytes 3076

commit v5 on v4

--- a/solution.py
+++ b/solution.py
@@ -381,7 +381,7 @@
     projected = result[...]
     scale = lax.rsqrt(jnp.mean(projected * projected, axis=-1, keepdims=True) + EPSILON)
     out_ref[...] = (
-        hid_ref[...].astype(jnp.float32) + projected * scale * gain_ref[...]
+        hid_ref[...].astype(jnp.float32) + projected * scale * gain_ref[...][None, :]
     ).astype(jnp.bfloat16)
 
 
@@ -434,12 +434,12 @@
     )(
         meta, heads, cache_keys, cache_values,
         np.concatenate([cosine, cosine], axis=1), np.concatenate([-sine, sine], axis=1),
-        ids_col, ids_row, w_own, w_across, own_rows, post_gain[None, :],
+        ids_col, ids_row, w_own, w_across, own_rows, post_gain,
     )
 
 
 def project_in_kernel(
-    selected, sizes, stretch, meta_ref, hid_ref, gain_ref, freq_ref, ids_ref,
+    selected, sizes, stretch, meta_ref, hid_ref, gain_ref, ids_ref,
     wq_hbm, wk_hbm, wv_hbm, wo_ref, heads_ref, wo_across_ref,
     normed, weights, ship, wq_ref, wk_ref, wv_ref, cos_ref, sin_ref,
     l_sem, x_send, x_recv, f_send, f_recv, s_send, s_recv, y_send, y_recv, w_send, w_recv, z_send, z_recv,
@@ -540,12 +540,15 @@
     def make_tables():
         layout = Layout(owners_ref, counts_ref, stretch)
         below = lax.broadcasted_iota(jnp.int32, (stretch, 1), 0)
+        step = lax.broadcasted_iota(jnp.int32, (1, HEAD), 1)
+        step = jnp.where(step < HEAD // 2, step, step - HEAD // 2).astype(jnp.float32)
+        frequency = jnp.exp(step * (-2.0 * math.log(ROPE_BASE) / HEAD))
         for i in range(cos_ref.shape[0] // stretch):
             row = below + (half * cos_ref.shape[0] + i * stretch)
             code = layout.of_queries(row - selected)
             if i == 0:
                 code = jnp.where(row < selected, layout.of_cached(ids_ref[...]), code)
-            angle = (code - request_base(code)).astype(jnp.float32) * freq_ref[...]
+            angle = (code - request_base(code)).astype(jnp.float32) * frequency
             sine = jnp.sin(angle)
             lane = lax.broadcasted_iota(jnp.int32, sine.shape, 1)
             cos_ref[pl.ds(i * stretch, stretch), :] = jnp.cos(angle)
@@ -613,7 +616,7 @@
     y_start(1)
     wide = hid_ref[...].astype(jnp.float32)
     scale = lax.rsqrt(jnp.mean(wide * wide, axis=-1, keepdims=True) + EPSILON)
-    normed[spot, pl.ds(mine, rows)] = (wide * scale * gain_ref[...]).astype(jnp.bfloat16)
+    normed[spot, pl.ds(mine, rows)] = (wide * scale * gain_ref[...][None, :]).astype(jnp.bfloat16)
     x_copy(0).start()
     x_copy(1).start()
     s_copy(0, spot).start()
@@ -647,6 +650,7 @@
     s_copy(1, left, twin).wait_recv()
     s_copy(2, right, twin).wait_recv()
     their_blocks(0, 1, 1, 3)
+    own_blocks(1, 2)
     for d in range(2):
         for j in range(2):
             g_copy(d, j, beyond).wait_recv()
@@ -667,7 +671,6 @@
     for n in range(4):
         w_copy(n, beyond, theirs_first + n).wait_recv()
     their_blocks(3, 4, 0, 4)
-    own_blocks(1, 2)
     o_copy(1, wo_across_ref, below, None, zs[0]).wait_recv()
     o_copy(3, wo_across_ref, below, 0, zs[0]).start()
     o_copy(2, wo_across_ref, above, None, zs[1]).wait_recv()
@@ -718,7 +721,7 @@
         out_shape=(
             jax.ShapeDtypeStruct((4, new_rows, HEAD), bf16), jax.ShapeDtypeStruct(w_out.shape, bf16)
         ),
-        in_specs=[smem] + [vmem] * 4 + [hbm] * 4,
+        in_specs=[smem] + [vmem] * 3 + [hbm] * 4,
         out_specs=(vmem, hbm),
         scratch_shapes=[
             pltpu.VMEM((AROUND, 2 * rows, features), bf16),
@@ -735,7 +738,7 @@
         ),
         name="project_in",
     )(
-        meta, own_rows, gain[None, :], np.concatenate([frequencies()] * 2)[None, :], ids_col,
+        meta, own_rows, gain, ids_col,
         w_query, w_key, w_value, w_out,
     )
 

time: 163 us -> 161 us (0.988)
  local copies, waits for them, and re-layouts: 7.96 us -> 5.95 us
    broadcast_in_dim x2 -> x0, local copies, waits for them, and re-layouts: 2.08 us -> none  [the longest x1 1.34 us: project(): post_gain[None, :]]
where the time goes in v5:
time: 161 us
  Pallas kernels  154 us (96%)
  local copies, waits for them, and re-layouts  5.95 us (4%)
    pallas_call x1, Pallas kernels, project_in(): pl.pallas_call(functools.partial(project_in_kernel, selected, sizes, stre...  79.5 us
    pallas_call x1, Pallas kernels, project(): pl.pallas_call(functools.partial(project_kernel, selected, sizes), out_sh...  74.4 us
    unnamed x11, local copies, waits for them, and re-layouts  4.37 us

profile of v5, /device:TPU:1, one launch (start us, length us, event | category | flops | bytes accessed | tf_op | source)
XLA Modules:
  0.0 160.6 jit_solution(4213015714880334110)
XLA Ops:
  0.0 0.8 reshape.3
  0.8 0.7 pad_add_fusion.meta_ref
  1.5 0.0 copy-start.3
  1.5 0.7 pad.4
  2.2 0.0 copy-start.4
  2.2 0.1 copy.16.ids_ref.ids_col_ref
  2.3 0.0 copy-start
  2.4 1.3 copy-done
  3.6 0.0 copy-start.2
  3.6 0.7 copy-done.2
  4.4 0.0 copy-start.1
  4.4 79.5 %project_in.1 = (bf16[4,2048,128]{2,1,0:T(8,128)(2,1)}, bf16[256,4608]{1,0:T(8,128)(2,1)}) custom-call(s32[75]{0:T(128)S(1)} %pad_add_fusion.meta_ref, bf16[128,4608]{1,0:T(8,128)(2,1)S(1)} %bitcast.8, f32[4608]{0:T(1024)S(1)} %copy-done.2, s32[256,1]{1,0:T(8,128)S(1)} %copy.16.ids_ref.ids_col_ref, bf16[4608,256]{1,0:T(8,128)(2,1)} %wq_hbm.1, ...), custom_call_target="tpu_custom_call" | custom-call | tf_op jit(solution)/shard_map/project_in/pallas_call | solution.py:719
  83.8 0.0 copy-done.3
  83.8 0.0 copy-done.4
  83.9 0.0 copy-done.1
  83.9 74.4 %project.1 = bf16[128,4608]{1,0:T(8,128)(2,1)} custom-call(s32[75]{0:T(128)} %copy-done.3, bf16[4,2048,128]{2,1,0:T(8,128)(2,1)} %get-tuple-element.7.heads_ref, bf16[8,256,128]{2,1,0:T(8,128)(2,1)} %ck_ref.1, bf16[8,256,128]{2,1,0:T(8,128)(2,1)} %cv_ref.1, f32[8,128]{1,0:T(8,128)} %constant.6.clone.pcos_ref, f32[8,128]{1,0:T(8,128)} %constant.7.clone.psin_ref, ...), custom_call_target="tpu_custom_call" | custom-call | tf_op jit(solution)/shard_map/project/pallas_call | solution.py:402
  158.3 2.4 %copy.19 = bf16[1,128,4608]{2,1,0:T(8,128)(2,1)} copy(bf16[1,128,4608]{2,1,0:T(8,128)(2,1)} %bitcast.9) | data formatting | bytes 2359296
Async XLA Ops:
  1.5 82.3 %copy-start.3 = (s32[75]{0:T(128)}, s32[75]{0:T(128)S(1)}, u32[]{:S(2)}) copy-start(s32[75]{0:T(128)S(1)} %pad_add_fusion.meta_ref) | copy-start | bytes 904
  2.2 81.6 %copy-start.4 = (s32[256]{0:T(256)}, s32[256]{0:T(256)S(1)}, u32[]{:S(2)}) copy-start(s32[256]{0:T(256)S(1)} %pad.4) | copy-start | bytes 3076
  2.3 1.3 copy-start
  3.6 0.7 copy-start.2
  4.4 79.5 %copy-start.1 = (s32[256,1]{1,0:T(8,128)}, s32[256,1]{1,0:T(8,128)S(1)}, u32[]{:S(2)}) copy-start(s32[256,1]{1,0:T(8,128)S(1)} %copy.16.ids_ref.ids_col_ref) | copy-start | bytes 3076
